TPU v7x, 32 devices: a whole 2x2x4 slice. The times are simulated.
32 devices in a mesh: fsdp: 4 (over y, x), ctx: 8 (over z, core).
Axes of the slice: x: 2, y: 2, z: 4, core: 2. Of those that a mesh axis runs over, the one named last changes fastest.
Arguments:
- inputs: bfloat16 [2, 8, 512, 768], P(None, 'fsdp', 'ctx'), may hold values from -6 to 6
- segments: int32 [2, 8, 512], P(None, 'fsdp', 'ctx'), may hold values from -1 to 2, as said below
- ln1_scale: bfloat16 [768], P('fsdp'), may hold values from 0.099609375 to 1.8984375
- ln1_bias: bfloat16 [768], P('fsdp'), may hold values from -1.75 to 1.75
- w_qkv: bfloat16 [768, 2304], P('fsdp'), may hold values from -0.21875 to 0.21875
- b_query: bfloat16 [768], P('fsdp'), may hold values from -1.75 to 1.75
- b_value: bfloat16 [768], P('fsdp'), may hold values from -1.75 to 1.75
- w_proj: bfloat16 [768, 768], P('fsdp'), may hold values from -2.5 to 2.5
- b_proj: bfloat16 [768], P('fsdp'), may hold values from -1.75 to 1.75
- ln2_scale: bfloat16 [768], P('fsdp'), may hold values from 0.099609375 to 1.8984375
- ln2_bias: bfloat16 [768], P('fsdp'), may hold values from -1.75 to 1.75
- w_up: bfloat16 [768, 3072], P('fsdp'), may hold values from -0.21875 to 0.21875
- b_up: bfloat16 [3072], P('fsdp'), may hold values from -1.75 to 1.75
- w_down: bfloat16 [3072, 768], P('fsdp'), may hold values from -0.109375 to 0.109375
- b_down: bfloat16 [768], P('fsdp'), may hold values from -1.75 to 1.75
- cotangent: bfloat16 [2, 8, 512, 768], P(None, 'fsdp', 'ctx'), may hold values from -6 to 6
Outputs:
- out: bfloat16 [2, 8, 512, 768], P(None, 'fsdp', 'ctx')
- d_input: bfloat16 [2, 8, 512, 768], P(None, 'fsdp', 'ctx')
- grad_ln1_scale: float32 [768], P('fsdp')
- grad_ln1_bias: float32 [768], P('fsdp')
- grad_w_qkv: float32 [768, 2304], P('fsdp')
- grad_b_query: float32 [768], P('fsdp')
- grad_b_value: float32 [768], P('fsdp')
- grad_w_proj: float32 [768, 768], P('fsdp')
- grad_b_proj: float32 [768], P('fsdp')
- grad_ln2_scale: float32 [768], P('fsdp')
- grad_ln2_bias: float32 [768], P('fsdp')
- grad_w_up: float32 [768, 3072], P('fsdp')
- grad_b_up: float32 [3072], P('fsdp')
- grad_w_down: float32 [3072, 768], P('fsdp')
- grad_b_down: float32 [768], P('fsdp')
Inputs may be any that keep to these rules, and one draw needn't show every extreme that they name: `segments`: along a sequence document numbers never fall until the padding (-1) that ends it. In every group of 2 consecutive sequences of a micro-batch, one sequence, drawn from the seed, is a single document numbered 0 with no padding; every other sequence ends in padding.
All inputs are finite; a program needn't handle non-finite values.
Results may differ from a plain program's by a relative error of at most 0.019.
Values may be sent and summed in bfloat16 or wider, within the bound.
A program may use at most 320 MiB of HBM per device.

v0:
```python
import jax
import jax.numpy as jnp
from jax import lax
from jax.sharding import PartitionSpec as P

HEADS = 12


NORM_EPS = 1e-06
SCORE_SCALE = 0.125
MASKED = -1e30


def layer_norm(values, scale_vec, bias_vec):
    center = values - jnp.mean(values, -1, keepdims=True)
    spread = jnp.mean(center * center, -1, keepdims=True)
    return center * lax.rsqrt(spread + NORM_EPS) * scale_vec + bias_vec


def gelu_tanh(values):
    return jax.nn.gelu(values, approximate=True)


def block_size(length_in, step_rows):
    blocked = step_rows
    while blocked * 2 <= 512 and length_in % (blocked * 2) == 0:
        blocked = blocked * 2
    return blocked


def to_heads(array, head_count):
    return array.reshape(array.shape[0], array.shape[1], head_count, -1)


def allowed_mask(seg_query, pos_query, seg_key, pos_key):
    same = seg_query[:, :, None] == seg_key[:, None, :]
    living = (seg_key[:, None, :] >= 0.0) | (pos_query[:, None] == pos_key[None, :])[None]
    return (same & living)[:, :, None, :]


def score_block(query_blk, key_blk, seg_query, pos_query, seg_key, pos_key):
    scores = (
        jnp.einsum("sqhd,skhd->sqhk", query_blk, key_blk, preferred_element_type=jnp.float32)
        * SCORE_SCALE
    )
    return (scores, allowed_mask(seg_query, pos_query, seg_key, pos_key))


def block_grads(
    query_blk,
    dout_blk,
    lse_blk,
    delta_blk,
    seg_query,
    pos_query,
    key_blk,
    value_blk,
    seg_key,
    pos_key,
):
    scores, allowed = score_block(query_blk, key_blk, seg_query, pos_query, seg_key, pos_key)
    probs = jnp.where(allowed, jnp.exp(scores - lse_blk[..., None]), 0.0)
    dprobs = jnp.einsum("sqhd,skhd->sqhk", dout_blk, value_blk, preferred_element_type=jnp.float32)
    dscores = (probs * (dprobs - delta_blk[..., None])).astype(jnp.bfloat16)
    return (dscores, probs.astype(jnp.bfloat16))


def key_side(
    query_blk,
    dout_blk,
    lse_blk,
    delta_blk,
    seg_query,
    pos_query,
    key_blk,
    value_blk,
    seg_key,
    pos_key,
):
    dscores, probs_low = block_grads(
        query_blk,
        dout_blk,
        lse_blk,
        delta_blk,
        seg_query,
        pos_query,
        key_blk,
        value_blk,
        seg_key,
        pos_key,
    )
    key_grad = (
        jnp.einsum("sqhk,sqhd->skhd", dscores, query_blk, preferred_element_type=jnp.float32)
        * SCORE_SCALE
    )
    value_grad = jnp.einsum(
        "sqhk,sqhd->skhd", probs_low, dout_blk, preferred_element_type=jnp.float32
    )
    return (key_grad, value_grad)


def contract_rows(left, right):
    return lax.dot_general(
        left, right, (((0,), (0,)), ((), ())), preferred_element_type=jnp.float32
    )


def contract_cols(left, right):
    return lax.dot_general(
        left, right, (((1,), (1,)), ((), ())), preferred_element_type=jnp.float32
    )


def per_device(
    inputs,
    segments,
    ln1_scale,
    ln1_bias,
    w_qkv,
    b_query,
    b_value,
    w_proj,
    b_proj,
    ln2_scale,
    ln2_bias,
    w_up,
    b_up,
    w_down,
    b_down,
    cotangent,
):
    micro_count, seq_dev, shard_len, model_width = inputs.shape
    head_count = HEADS
    head_width = model_width // head_count
    row_count = seq_dev * shard_len
    place = lax.axis_index("ctx")
    pos_local = place * shard_len + lax.iota(jnp.int32, shard_len)
    owned = (
        ln1_scale,
        ln1_bias,
        w_qkv,
        b_query,
        b_value,
        w_proj,
        b_proj,
        ln2_scale,
        ln2_bias,
        w_up,
        b_up,
        w_down,
        b_down,
    )
    summed_shards = None
    outputs_list = []
    input_grads = []
    for batch_num in range(micro_count):
        gathered = (
            lax.all_gather(owned[0], "fsdp", axis=0, tiled=True),
            lax.all_gather(owned[1], "fsdp", axis=0, tiled=True),
            lax.all_gather(owned[2], "fsdp", axis=0, tiled=True),
            lax.all_gather(owned[3], "fsdp", axis=0, tiled=True),
            lax.all_gather(owned[4], "fsdp", axis=0, tiled=True),
            lax.all_gather(owned[5], "fsdp", axis=0, tiled=True),
            lax.all_gather(owned[6], "fsdp", axis=0, tiled=True),
            lax.all_gather(owned[7], "fsdp", axis=0, tiled=True),
            lax.all_gather(owned[8], "fsdp", axis=0, tiled=True),
            lax.all_gather(owned[9], "fsdp", axis=0, tiled=True),
            lax.all_gather(owned[10], "fsdp", axis=0, tiled=True),
            lax.all_gather(owned[11], "fsdp", axis=0, tiled=True),
            lax.all_gather(owned[12], "fsdp", axis=0, tiled=True),
        )
        (
            gain_one,
            shift_one,
            w_qkv_all,
            bias_query,
            bias_value,
            w_proj_all,
            bias_proj,
            gain_two,
            shift_two,
            w_up_all,
            bias_up,
            w_down_all,
            bias_down,
        ) = gathered
        x_rows = inputs[batch_num].reshape(row_count, model_width).astype(jnp.float32)
        seg_local = segments[batch_num].astype(jnp.float32)
        cot_rows = cotangent[batch_num].reshape(row_count, model_width)
        normed_one, norm_one_pull = jax.vjp(
            layer_norm, x_rows, gain_one.astype(jnp.float32), shift_one.astype(jnp.float32)
        )
        hidden_one = normed_one.astype(jnp.bfloat16)
        projected = jnp.dot(hidden_one, w_qkv_all, preferred_element_type=jnp.float32)
        queries = (projected[:, :model_width] + bias_query.astype(jnp.float32)).astype(jnp.bfloat16)
        keys_loc = projected[:, model_width : 2 * model_width].astype(jnp.bfloat16)
        values_loc = (projected[:, 2 * model_width :] + bias_value.astype(jnp.float32)).astype(
            jnp.bfloat16
        )
        query_heads = queries.reshape(seq_dev, shard_len, head_count, head_width)
        shipped = (
            keys_loc.reshape(seq_dev, shard_len, model_width),
            values_loc.reshape(seq_dev, shard_len, model_width),
            seg_local.astype(jnp.bfloat16),
        )
        stat_shape = (seq_dev, shard_len, head_count)
        start_state = (
            jnp.full(stat_shape, MASKED, jnp.float32),
            jnp.zeros(stat_shape, jnp.float32),
            jnp.zeros((seq_dev, shard_len, head_count, head_width), jnp.float32),
        )
        key_part = lax.all_gather(shipped[0], "ctx", axis=1, tiled=True)
        value_part = lax.all_gather(shipped[1], "ctx", axis=1, tiled=True)
        seg_part = lax.all_gather(shipped[2], "ctx", axis=1, tiled=True)
        length_in = key_part.shape[1]
        step_len = block_size(length_in, shard_len)

        def forward_inner(turn, state):
            row_max, row_sum, weighted = state
            begin = turn * step_len
            key_blk = to_heads(lax.dynamic_slice_in_dim(key_part, begin, step_len, 1), head_count)
            value_blk = to_heads(
                lax.dynamic_slice_in_dim(value_part, begin, step_len, 1), head_count
            )
            seg_blk = lax.dynamic_slice_in_dim(seg_part, begin, step_len, 1).astype(jnp.float32)
            pos_blk = begin + lax.iota(jnp.int32, step_len)
            scores, allowed = score_block(
                query_heads, key_blk, seg_local, pos_local, seg_blk, pos_blk
            )
            scores = jnp.where(allowed, scores, MASKED)
            new_max = jnp.maximum(row_max, jnp.max(scores, -1))
            expo = jnp.where(allowed, jnp.exp(scores - new_max[..., None]), 0.0)
            factor = jnp.exp(row_max - new_max)
            row_sum = row_sum * factor + jnp.sum(expo, -1)
            weighted = weighted * factor[..., None] + jnp.einsum(
                "sqhk,skhd->sqhd",
                expo.astype(jnp.bfloat16),
                value_blk,
                preferred_element_type=jnp.float32,
            )
            return (new_max, row_sum, weighted)

        row_max, row_sum, weighted = lax.fori_loop(
            0, length_in // step_len, forward_inner, start_state
        )
        attended = weighted / row_sum[..., None]
        log_sum = row_max + jnp.log(row_sum)
        mixed = attended.reshape(row_count, model_width).astype(jnp.bfloat16)
        resid = (
            x_rows
            + jnp.dot(mixed, w_proj_all, preferred_element_type=jnp.float32)
            + bias_proj.astype(jnp.float32)
        )
        normed_two, norm_two_pull = jax.vjp(
            layer_norm, resid, gain_two.astype(jnp.float32), shift_two.astype(jnp.float32)
        )
        hidden_two = normed_two.astype(jnp.bfloat16)
        pre_act = jnp.dot(
            hidden_two, w_up_all, preferred_element_type=jnp.float32
        ) + bias_up.astype(jnp.float32)
        activ, gelu_pull = jax.vjp(gelu_tanh, pre_act)
        activ_low = activ.astype(jnp.bfloat16)
        result = (
            resid
            + jnp.dot(activ_low, w_down_all, preferred_element_type=jnp.float32)
            + bias_down.astype(jnp.float32)
        )
        outputs_list.append(result.astype(jnp.bfloat16).reshape(seq_dev, shard_len, model_width))
        d_activ = contract_cols(cot_rows, w_down_all)
        grad_down = contract_rows(activ_low, cot_rows)
        grad_bias_down = jnp.sum(cot_rows.astype(jnp.float32), 0)
        d_pre = gelu_pull(d_activ)[0].astype(jnp.bfloat16)
        grad_up = contract_rows(hidden_two, d_pre)
        grad_bias_up = jnp.sum(d_pre.astype(jnp.float32), 0)
        d_hidden_two = contract_cols(d_pre, w_up_all)
        d_resid_part, grad_gain_two, grad_shift_two = norm_two_pull(d_hidden_two)
        d_resid = cot_rows.astype(jnp.float32) + d_resid_part
        d_branch = d_resid.astype(jnp.bfloat16)
        grad_proj = contract_rows(mixed, d_branch)
        grad_bias_proj = jnp.sum(d_branch.astype(jnp.float32), 0)
        d_mixed = contract_cols(d_branch, w_proj_all).astype(jnp.bfloat16)
        dout_heads = d_mixed.reshape(seq_dev, shard_len, head_count, head_width)
        delta = jnp.sum(dout_heads.astype(jnp.float32) * attended, -1)
        zero_heads = jnp.zeros((seq_dev, shard_len, head_count, head_width), jnp.float32)
        key_all, value_all, seg_all = (
            lax.all_gather(shipped[0], "ctx", axis=1, tiled=True),
            lax.all_gather(shipped[1], "ctx", axis=1, tiled=True),
            lax.all_gather(shipped[2], "ctx", axis=1, tiled=True),
        )
        query_key_part = key_all
        query_value_part = value_all
        query_seg_part = seg_all
        query_length_in = query_key_part.shape[1]
        query_step_len = block_size(query_length_in, shard_len)

        def query_inner(turn, grad_in):
            begin = turn * query_step_len
            key_blk = to_heads(
                lax.dynamic_slice_in_dim(query_key_part, begin, query_step_len, 1), head_count
            )
            value_blk = to_heads(
                lax.dynamic_slice_in_dim(query_value_part, begin, query_step_len, 1), head_count
            )
            seg_blk = lax.dynamic_slice_in_dim(query_seg_part, begin, query_step_len, 1).astype(
                jnp.float32
            )
            pos_blk = 0 + begin + lax.iota(jnp.int32, query_step_len)
            dscores, probs_low = block_grads(
                query_heads,
                dout_heads,
                log_sum,
                delta,
                seg_local,
                pos_local,
                key_blk,
                value_blk,
                seg_blk,
                pos_blk,
            )
            return (
                grad_in
                + jnp.einsum(
                    "sqhk,skhd->sqhd", dscores, key_blk, preferred_element_type=jnp.float32
                )
                * SCORE_SCALE
            )

        query_grad = lax.fori_loop(0, query_length_in // query_step_len, query_inner, zero_heads)
        rows_in = shard_len * lax.axis_size("ctx")
        key_step_len = block_size(rows_in, shard_len)

        def one_block(turn):
            begin = turn * key_step_len
            key_blk = to_heads(
                lax.dynamic_slice_in_dim(key_all, begin, key_step_len, 1), head_count
            )
            value_blk = to_heads(
                lax.dynamic_slice_in_dim(value_all, begin, key_step_len, 1), head_count
            )
            seg_blk = lax.dynamic_slice_in_dim(seg_all, begin, key_step_len, 1).astype(jnp.float32)
            pos_blk = begin + lax.iota(jnp.int32, key_step_len)
            key_grad, value_grad = key_side(
                query_heads,
                dout_heads,
                log_sum,
                delta,
                seg_local,
                pos_local,
                key_blk,
                value_blk,
                seg_blk,
                pos_blk,
            )
            joined = jnp.stack(
                (
                    key_grad.reshape(seq_dev, key_step_len, model_width),
                    value_grad.reshape(seq_dev, key_step_len, model_width),
                ),
                2,
            )
            return joined.transpose(1, 0, 2, 3).reshape(key_step_len, seq_dev * 2 * model_width)

        blocks = lax.map(one_block, jnp.arange(rows_in // key_step_len, dtype=jnp.int32))
        own_terms = lax.psum_scatter(
            blocks.reshape(rows_in, seq_dev * 2 * model_width).astype(jnp.bfloat16),
            "ctx",
            scatter_dimension=0,
            tiled=True,
        ).astype(jnp.float32)
        own_terms = own_terms.reshape(shard_len, seq_dev, 2, model_width).transpose(1, 2, 0, 3)
        key_grad = own_terms[:, 0]
        value_grad = own_terms[:, 1]
        query_low = query_grad.reshape(row_count, model_width).astype(jnp.bfloat16)
        key_low = key_grad.reshape(row_count, model_width).astype(jnp.bfloat16)
        value_low = value_grad.reshape(row_count, model_width).astype(jnp.bfloat16)
        d_qkv = jnp.concatenate((query_low, key_low, value_low), 1)
        grad_qkv = contract_rows(hidden_one, d_qkv)
        grad_bias_query = jnp.sum(query_low.astype(jnp.float32), 0)
        grad_bias_value = jnp.sum(value_low.astype(jnp.float32), 0)
        d_hidden_one = contract_cols(d_qkv, w_qkv_all)
        d_input_part, grad_gain_one, grad_shift_one = norm_one_pull(d_hidden_one)
        input_grads.append(
            (d_resid + d_input_part).astype(jnp.bfloat16).reshape(seq_dev, shard_len, model_width)
        )
        local_grads = (
            grad_gain_one,
            grad_shift_one,
            grad_qkv,
            grad_bias_query,
            grad_bias_value,
            grad_proj,
            grad_bias_proj,
            grad_gain_two,
            grad_shift_two,
            grad_up,
            grad_bias_up,
            grad_down,
            grad_bias_down,
        )
        shard_part = (
            lax.psum_scatter(
                local_grads[0].astype(jnp.bfloat16), "fsdp", scatter_dimension=0, tiled=True
            ).astype(jnp.float32),
            lax.psum_scatter(
                local_grads[1].astype(jnp.bfloat16), "fsdp", scatter_dimension=0, tiled=True
            ).astype(jnp.float32),
            lax.psum_scatter(
                local_grads[2].astype(jnp.bfloat16), "fsdp", scatter_dimension=0, tiled=True
            ).astype(jnp.float32),
            lax.psum_scatter(
                local_grads[3].astype(jnp.bfloat16), "fsdp", scatter_dimension=0, tiled=True
            ).astype(jnp.float32),
            lax.psum_scatter(
                local_grads[4].astype(jnp.bfloat16), "fsdp", scatter_dimension=0, tiled=True
            ).astype(jnp.float32),
            lax.psum_scatter(
                local_grads[5].astype(jnp.bfloat16), "fsdp", scatter_dimension=0, tiled=True
            ).astype(jnp.float32),
            lax.psum_scatter(
                local_grads[6].astype(jnp.bfloat16), "fsdp", scatter_dimension=0, tiled=True
            ).astype(jnp.float32),
            lax.psum_scatter(
                local_grads[7].astype(jnp.bfloat16), "fsdp", scatter_dimension=0, tiled=True
            ).astype(jnp.float32),
            lax.psum_scatter(
                local_grads[8].astype(jnp.bfloat16), "fsdp", scatter_dimension=0, tiled=True
            ).astype(jnp.float32),
            lax.psum_scatter(
                local_grads[9].astype(jnp.bfloat16), "fsdp", scatter_dimension=0, tiled=True
            ).astype(jnp.float32),
            lax.psum_scatter(
                local_grads[10].astype(jnp.bfloat16), "fsdp", scatter_dimension=0, tiled=True
            ).astype(jnp.float32),
            lax.psum_scatter(
                local_grads[11].astype(jnp.bfloat16), "fsdp", scatter_dimension=0, tiled=True
            ).astype(jnp.float32),
            lax.psum_scatter(
                local_grads[12].astype(jnp.bfloat16), "fsdp", scatter_dimension=0, tiled=True
            ).astype(jnp.float32),
        )
        shard_part = (
            lax.psum(shard_part[0].astype(jnp.bfloat16), "ctx").astype(jnp.float32),
            lax.psum(shard_part[1].astype(jnp.bfloat16), "ctx").astype(jnp.float32),
            lax.psum(shard_part[2].astype(jnp.bfloat16), "ctx").astype(jnp.float32),
            lax.psum(shard_part[3].astype(jnp.bfloat16), "ctx").astype(jnp.float32),
            lax.psum(shard_part[4].astype(jnp.bfloat16), "ctx").astype(jnp.float32),
            lax.psum(shard_part[5].astype(jnp.bfloat16), "ctx").astype(jnp.float32),
            lax.psum(shard_part[6].astype(jnp.bfloat16), "ctx").astype(jnp.float32),
            lax.psum(shard_part[7].astype(jnp.bfloat16), "ctx").astype(jnp.float32),
            lax.psum(shard_part[8].astype(jnp.bfloat16), "ctx").astype(jnp.float32),
            lax.psum(shard_part[9].astype(jnp.bfloat16), "ctx").astype(jnp.float32),
            lax.psum(shard_part[10].astype(jnp.bfloat16), "ctx").astype(jnp.float32),
            lax.psum(shard_part[11].astype(jnp.bfloat16), "ctx").astype(jnp.float32),
            lax.psum(shard_part[12].astype(jnp.bfloat16), "ctx").astype(jnp.float32),
        )
        if summed_shards is None:
            summed_shards = shard_part
        else:
            summed_shards = tuple((old + new for old, new in zip(summed_shards, shard_part)))
    return (jnp.stack(outputs_list), jnp.stack(input_grads)) + tuple(summed_shards)


def solution(mesh):
    placed = (
        P(None, "fsdp", "ctx", None),
        P(None, "fsdp", "ctx"),
        P("fsdp"),
        P("fsdp"),
        P("fsdp", None),
        P("fsdp"),
        P("fsdp"),
        P("fsdp", None),
        P("fsdp"),
        P("fsdp"),
        P("fsdp"),
        P("fsdp", None),
        P("fsdp"),
        P("fsdp", None),
        P("fsdp"),
        P(None, "fsdp", "ctx", None),
    )
    return jax.shard_map(
        per_device,
        mesh=mesh,
        in_specs=placed,
        out_specs=(
            P(None, "fsdp", "ctx", None),
            P(None, "fsdp", "ctx", None),
            P("fsdp"),
            P("fsdp"),
            P("fsdp", None),
            P("fsdp"),
            P("fsdp"),
            P("fsdp", None),
            P("fsdp"),
            P("fsdp"),
            P("fsdp"),
            P("fsdp", None),
            P("fsdp"),
            P("fsdp", None),
            P("fsdp"),
        ),
        check_vma=False,
    )
```

profile of v0, /device:TPU:1, one launch (start us, length us, event | category | flops | bytes accessed | tf_op | source)
XLA Modules:
  0.0 1005.8 jit_solution(3049105654457366133)
XLA Ops:
  11.7 13.8 %all-reduce.29 = (bf16[768]{0:T(1024)(128)(2,1)S(1)}, bf16[768]{0:T(1024)(128)(2,1)S(1)}, bf16[768]{0:T(1024)(128)(2,1)S(1)}, bf16[768]{0:T(1024)(128)(2,1)S(1)}...) all-reduce(bf16[768]{0:T(1024)(128)(2,1)S(1)} %dynamic-update-slice, ...), channel_id=1, replica_groups=mesh['fsdp'=4,'ctx'=8] {'fsdp'}, use_global_device_ids=true, to_apply=%add.1 | all-reduce | flops 5376 | bytes 21504
  27.9 31.5 %all-gather.12.cloned.1.call-done = bf16[768,2304]{1,0:T(8,128)(2,1)} async-done(((bf16[192,2304]{1,0:T(8,128)(2,1)}), bf16[768,2304]{1,0:T(8,128)(2,1)}) %all-gather.12.cloned.1.call-update) | async-done | bytes 3538960 | tf_op jit(solution)/shard_map/all_gather | solution.py:160
  59.4 2.9 fusion.125
  67.1 1.8 slice.126
  71.1 12.2 %all-gather.2 = bf16[8,64,2]{1,2,0:T(2,128)(2,1)S(1)} all-gather(bf16[1,64,2]{1,2,0:T(2,128)(2,1)S(1)} %get-tuple-element.339), channel_id=1, replica_groups=mesh['fsdp'=4,'ctx'=8] {'ctx'}, dimensions={0}, use_global_device_ids=true | all-gather | bytes 2304 | tf_op jit(solution)/shard_map/all_gather | solution.py:214
  83.4 8.6 all-gather
  92.2 7.2 all-gather.1
  104.8 13.7 %all-gather.22.cloned.1.call-done = bf16[3072,768]{1,0:T(8,128)(2,1)} async-done(((bf16[768,768]{1,0:T(8,128)(2,1)}), bf16[3072,768]{1,0:T(8,128)(2,1)}) %all-gather.22.cloned.1.call-update) | async-done | bytes 4718608 | tf_op jit(solution)/shard_map/all_gather | solution.py:169
  118.5 5.3 fusion.127
  123.8 2.8 fusion.128
  126.5 19.1 %all-gather.14.cloned.1.call-done = bf16[2,512,768]{2,1,0:T(8,128)(2,1)} async-done(((bf16[2,64,768]{2,1,0:T(8,128)(2,1)}), bf16[2,512,768]{2,1,0:T(8,128)(2,1)}) %all-gather.14.cloned.1.call-update) | async-done | bytes 1572880 | tf_op jit(solution)/shard_map/all_gather | solution.py:212
  145.6 1.7 copy.152
  147.3 24.9 %all-gather.16.cloned.1.call-done = bf16[2,512,768]{2,1,0:T(8,128)(2,1)} async-done(((bf16[2,64,768]{2,1,0:T(8,128)(2,1)}), bf16[2,512,768]{2,1,0:T(8,128)(2,1)}) %all-gather.16.cloned.1.call-update) | async-done | bytes 1572880 | tf_op jit(solution)/shard_map/all_gather | solution.py:213
  172.2 1.7 copy.155
  174.0 2.2 fusion.8
  178.0 2.1 fusion.120
  181.3 17.0 %all-gather.24.cloned.1.call-done = bf16[2,512,768]{2,1,0:T(8,128)(2,1)} async-done(((bf16[2,64,768]{2,1,0:T(8,128)(2,1)}), bf16[2,512,768]{2,1,0:T(8,128)(2,1)}) %all-gather.24.cloned.1.call-update) | async-done | bytes 1572880 | tf_op jit(solution)/shard_map/all_gather | solution.py:212
  198.3 2.6 copy.158
  200.9 24.1 %all-gather.26.cloned.1.call-done = bf16[2,512,768]{2,1,0:T(8,128)(2,1)} async-done(((bf16[2,64,768]{2,1,0:T(8,128)(2,1)}), bf16[2,512,768]{2,1,0:T(8,128)(2,1)}) %all-gather.26.cloned.1.call-update) | async-done | bytes 1572880 | tf_op jit(solution)/shard_map/all_gather | solution.py:213
  225.0 3.1 copy.161
  228.1 2.2 fusion.9
  231.9 2.0 fusion.119
  235.2 18.5 %all-gather.18.cloned.1.call-done = bf16[768,768]{1,0:T(8,128)(2,1)} async-done(((bf16[192,768]{1,0:T(8,128)(2,1)}), bf16[768,768]{1,0:T(8,128)(2,1)}) %all-gather.18.cloned.1.call-update) | async-done | bytes 1179664 | tf_op jit(solution)/shard_map/all_gather | solution.py:163
  253.7 2.0 fusion.121
  259.7 52.9 %all-gather.20.cloned.1.call-done = bf16[768,3072]{1,0:T(8,128)(2,1)} async-done(((bf16[192,3072]{1,0:T(8,128)(2,1)}), bf16[768,3072]{1,0:T(8,128)(2,1)}) %all-gather.20.cloned.1.call-update) | async-done | bytes 4718608 | tf_op jit(solution)/shard_map/all_gather | solution.py:167
  312.6 6.8 fusion.110
  321.2 3.7 fusion.108
  325.0 2.3 multiply_reduce_fusion.3
  331.5 2.1 reshape.527
  333.6 2.1 copy.165
  337.1 3.1 convolution_convert_fusion.7
  343.2 2.0 pad_maximum_fusion
  345.2 4.6 copy.191
  351.1 1.8 fusion.114
  353.5 2.5 convolution_convert_fusion.10
  356.0 2.1 reshape.528
  358.1 2.1 copy.178
  361.6 2.7 fusion.1
  366.8 3.1 copy.193
  374.2 3.7 convolution_convert_fusion.3
  379.2 3.7 convolution_convert_fusion.2
  384.4 3.7 convolution_convert_fusion.1
  389.7 3.7 convolution_convert_fusion
  398.4 31.0 %reduce-scatter.33.cloned.1.call-done = bf16[64,3072]{1,0:T(8,128)(2,1)} async-done(((bf16[512,3072]{1,0:T(8,128)(2,1)}), bf16[64,3072]{1,0:T(8,128)(2,1)}) %reduce-scatter.33.cloned.1.call-update) | async-done | bytes 393232
  431.3 2.7 slice_reduce_fusion.2
  435.0 3.0 convolution_convert_fusion.5
  443.1 2.9 convolution_convert_fusion.4
  450.1 2.5 fusion.86
  452.7 1.9 multiply_reduce_fusion.8
  456.3 6.3 reduce-scatter.19.cloned.1.call-done
  462.5 31.3 %reduce-scatter.21.cloned.1.call-done = bf16[192,768]{1,0:T(8,128)(2,1)} async-done(((bf16[768,768]{1,0:T(8,128)(2,1)}), bf16[192,768]{1,0:T(8,128)(2,1)}) %reduce-scatter.21.cloned.1.call-update) | async-done | bytes 294928 | tf_op jit(solution)/shard_map/reduce_scatter | solution.py:416
  493.8 60.1 %reduce-scatter.23.cloned.1.call-done = bf16[192,3072]{1,0:T(8,128)(2,1)} async-done(((bf16[768,3072]{1,0:T(8,128)(2,1)}), bf16[192,3072]{1,0:T(8,128)(2,1)}) %reduce-scatter.23.cloned.1.call-update) | async-done | bytes 1179664 | tf_op jit(solution)/shard_map/reduce_scatter | solution.py:428
  554.0 60.0 %reduce-scatter.25.cloned.1.call-done = bf16[192,3072]{1,0:T(8,128)(2,1)} async-done(((bf16[768,3072]{1,0:T(8,128)(2,1)}), bf16[192,3072]{1,0:T(8,128)(2,1)}) %reduce-scatter.25.cloned.1.call-update) | async-done | bytes 1179664 | tf_op jit(solution)/shard_map/reduce_scatter | solution.py:428
  614.0 60.0 %reduce-scatter.27.cloned.1.call-done = bf16[768,768]{1,0:T(8,128)(2,1)} async-done(((bf16[3072,768]{1,0:T(8,128)(2,1)}), bf16[768,768]{1,0:T(8,128)(2,1)}) %reduce-scatter.27.cloned.1.call-update) | async-done | bytes 1179664 | tf_op jit(solution)/shard_map/reduce_scatter | solution.py:434
  673.9 60.0 %reduce-scatter.29.cloned.1.call-done = bf16[768,768]{1,0:T(8,128)(2,1)} async-done(((bf16[3072,768]{1,0:T(8,128)(2,1)}), bf16[768,768]{1,0:T(8,128)(2,1)}) %reduce-scatter.29.cloned.1.call-update) | async-done | bytes 1179664 | tf_op jit(solution)/shard_map/reduce_scatter | solution.py:434
  733.9 50.2 %reduce-scatter.15.cloned.1.call-done = bf16[192,2304]{1,0:T(8,128)(2,1)} async-done(((bf16[768,2304]{1,0:T(8,128)(2,1)}), bf16[192,2304]{1,0:T(8,128)(2,1)}) %reduce-scatter.15.cloned.1.call-update) | async-done | bytes 884752 | tf_op jit(solution)/shard_map/reduce_scatter | solution.py:407
  784.1 50.2 %reduce-scatter.17.cloned.1.call-done = bf16[192,2304]{1,0:T(8,128)(2,1)} async-done(((bf16[768,2304]{1,0:T(8,128)(2,1)}), bf16[192,2304]{1,0:T(8,128)(2,1)}) %reduce-scatter.17.cloned.1.call-update) | async-done | bytes 884752 | tf_op jit(solution)/shard_map/reduce_scatter | solution.py:407
  835.7 13.6 %all-reduce.28 = (bf16[768]{0:T(1024)(128)(2,1)}, bf16[768]{0:T(1024)(128)(2,1)}, bf16[768]{0:T(1024)(128)(2,1)}, bf16[768]{0:T(1024)(128)(2,1)}, bf16[768]{0:T(...) all-reduce(bf16[768]{0:T(1024)(128)(2,1)} %copy-done.100, ...), channel_id=1, replica_groups=mesh['fsdp'=4,'ctx'=8] {'fsdp'}, use_global_device_ids=true, to_apply=%add.7 | all-reduce | flops 19200 | bytes 76800
  871.3 27.6 %all-reduce.26 = (bf16[192]{0:T(256)(128)(2,1)}, bf16[192]{0:T(256)(128)(2,1)}, bf16[192]{0:T(256)(128)(2,1)}, bf16[192]{0:T(256)(128)(2,1)}, bf16[192]{0:T(256)...) all-reduce(bf16[192]{0:T(256)(128)(2,1)} %dynamic-slice.11, ...), channel_id=1, replica_groups=mesh['fsdp'=4,'ctx'=8] {'ctx'}, use_global_device_ids=true, to_apply=%region_29.30 | all-reduce | flops 4608 | bytes 18432 | tf_op jit(solution)/shard_map/psum | solution.py:442
  899.0 1.8 add_convert_fusion.1
  901.5 3.5 fusion.72
  912.4 78.7 %all-reduce.32.cloned.1.call-done = (bf16[192,2304]{1,0:T(8,128)(2,1)}, bf16[192,2304]{1,0:T(8,128)(2,1)}, bf16[192,768]{1,0:T(8,128)(2,1)}, bf16[192,768]{1,0:T...) async-done(((bf16[192,2304]{1,0:T(8,128)(2,1)}, bf16[192,2304]{1,0:T(8,128)(2,1)}, ...) | async-done | bytes 7077904 | tf_op jit(solution)/shard_map/psum | solution.py:444
  991.1 3.4 convert_add_fusion
  994.5 1.7 convert_add_fusion.1
  (498 shorter events, 103.7 us)
Async XLA Ops:
  7.2 4.0 copy-start.146
  7.3 4.3 copy-start.147
  7.3 18.2 %copy-start.8 = (bf16[2,2,64,768]{3,2,1,0:T(8,128)(2,1)S(1)}, bf16[2,2,64,768]{3,2,1,0:T(8,128)(2,1)}, u32[]{:S(2)}) copy-start(bf16[2,2,64,768]{3,2,1,0:T(8,128)(2,1)} %param.16) | copy-start | bytes 1179652
  7.3 52.1 %all-gather.12.cloned.1.call-start = ((), (), s32[]{:S(2)}) async-start(), calls=%async_computation.10 | async-start | bytes 4423680 | tf_op jit(solution)/shard_map/all_gather | solution.py:160
  8.0 110.5 %all-gather.22.cloned.1.call-start = ((), (), s32[]{:S(2)}) async-start(), calls=%async_computation.15 | async-start | bytes 5898240 | tf_op jit(solution)/shard_map/all_gather | solution.py:169
  8.8 136.8 %all-gather.14.cloned.1.call-start = ((), (), s32[]{:S(2)}) async-start(), calls=%async_computation.11 | async-start | bytes 1769472 | tf_op jit(solution)/shard_map/all_gather | solution.py:212
  25.7 33.7 %copy-start.101 = (f32[128]{0:T(128)}, f32[128]{0:T(128)S(1)}, u32[]{:S(2)}) copy-start(f32[128]{0:T(128)S(1)} %div.100) | copy-start | bytes 1540
  25.8 33.6 %copy-start.103 = (f32[128]{0:T(128)}, f32[128]{0:T(128)S(1)}, u32[]{:S(2)}) copy-start(f32[128]{0:T(128)S(1)} %div.93) | copy-start | bytes 1540
  26.8 32.7 %copy-start.105 = (f32[128]{0:T(128)}, f32[128]{0:T(128)S(1)}, u32[]{:S(2)}) copy-start(f32[128]{0:T(128)S(1)} %rsqrt.40) | copy-start | bytes 1540
  26.8 32.6 %copy-start.150 = (f32[128]{0:T(128)}, f32[128]{0:T(128)S(1)}, u32[]{:S(2)}) copy-start(f32[128]{0:T(128)S(1)} %add.482) | copy-start | bytes 1540
  26.9 32.6 %copy-start.107 = (f32[128]{0:T(128)}, f32[128]{0:T(128)S(1)}, u32[]{:S(2)}) copy-start(f32[128]{0:T(128)S(1)} %rsqrt.42) | copy-start | bytes 1540
  59.4 4.7 copy-start.6
  64.1 108.2 %all-gather.16.cloned.1.call-start = ((), (), s32[]{:S(2)}) async-start(), calls=%async_computation.12 | async-start | bytes 1769472 | tf_op jit(solution)/shard_map/all_gather | solution.py:213
  67.0 4.1 copy-start.115
  67.0 25.1 %copy-start.113 = (bf16[768]{0:T(1024)(128)(2,1)S(1)}, bf16[768]{0:T(1024)(128)(2,1)}, u32[]{:S(2)}) copy-start(bf16[768]{0:T(1024)(128)(2,1)} %get-tuple-element.290) | copy-start | bytes 4612
  67.0 25.1 %copy-start.112 = (bf16[768]{0:T(1024)(128)(2,1)S(1)}, bf16[768]{0:T(1024)(128)(2,1)}, u32[]{:S(2)}) copy-start(bf16[768]{0:T(1024)(128)(2,1)} %get-tuple-element.292) | copy-start | bytes 4612
  67.0 25.1 %copy-start.111 = (bf16[768]{0:T(1024)(128)(2,1)S(1)}, bf16[768]{0:T(1024)(128)(2,1)}, u32[]{:S(2)}) copy-start(bf16[768]{0:T(1024)(128)(2,1)} %get-tuple-element.291) | copy-start | bytes 4612
  67.0 25.1 %copy-start.116 = (bf16[768]{0:T(1024)(128)(2,1)S(1)}, bf16[768]{0:T(1024)(128)(2,1)}, u32[]{:S(2)}) copy-start(bf16[768]{0:T(1024)(128)(2,1)} %param.28) | copy-start | bytes 4612
  67.0 33.9 %copy-start.84 = (bf16[2,2,64,768]{3,2,1,0:T(8,128)(2,1)S(1)}, bf16[2,2,64,768]{3,2,1,0:T(8,128)(2,1)}, u32[]{:S(2)}) copy-start(bf16[2,2,64,768]{3,2,1,0:T(8,128)(2,1)} %param.31) | copy-start | bytes 1179652
  67.1 131.3 %all-gather.24.cloned.1.call-start = ((), (), s32[]{:S(2)}) async-start(), calls=%async_computation.16 | async-start | bytes 1769472 | tf_op jit(solution)/shard_map/all_gather | solution.py:212
  68.9 32.6 %copy-start.9 = (bf16[2,2,64,768]{3,2,1,0:T(8,128)(2,1)S(1)}, bf16[2,2,64,768]{3,2,1,0:T(8,128)(2,1)}, u32[]{:S(2)}) copy-start(bf16[2,2,64,768]{3,2,1,0:T(8,128)(2,1)} %param.16) | copy-start | bytes 1179652
  69.0 156.0 %all-gather.26.cloned.1.call-start = ((), (), s32[]{:S(2)}) async-start(), calls=%async_computation.17 | async-start | bytes 1769472 | tf_op jit(solution)/shard_map/all_gather | solution.py:213
  69.5 184.2 %all-gather.18.cloned.1.call-start = ((), (), s32[]{:S(2)}) async-start(), calls=%async_computation.13 | async-start | bytes 1474560 | tf_op jit(solution)/shard_map/all_gather | solution.py:163
  70.3 242.3 %all-gather.20.cloned.1.call-start = ((), (), s32[]{:S(2)}) async-start(), calls=%async_computation.14 | async-start | bytes 5898240 | tf_op jit(solution)/shard_map/all_gather | solution.py:167
  71.0 325.4 %reduce-scatter.31.cloned.1.call-start = ((), (), s32[]{:S(2)}) async-start(), calls=%async_computation.26 | async-start | bytes 3538944
  101.6 16.9 %copy-start.33 = (bf16[1,2,64,768]{3,2,1,0:T(8,128)(2,1)}, bf16[1,2,64,768]{3,2,1,0:T(8,128)(2,1)S(1)}, u32[]{:S(2)}) copy-start(bf16[1,2,64,768]{3,2,1,0:T(8,128)(2,1)S(1)} %get-tuple-element.314) | copy-start | bytes 589828
  101.6 22.2 %copy-start.30 = (bf16[1,2,64,768]{3,2,1,0:T(8,128)(2,1)}, bf16[1,2,64,768]{3,2,1,0:T(8,128)(2,1)S(1)}, u32[]{:S(2)}) copy-start(bf16[1,2,64,768]{3,2,1,0:T(8,128)(2,1)S(1)} %get-tuple-element.313) | copy-start | bytes 589828
  104.8 123.3 %copy-start.44 = (bf16[2,64,12,64]{1,3,2,0:T(8,128)(2,1)}, bf16[2,64,12,64]{1,3,2,0:T(8,128)(2,1)S(1)}, u32[]{:S(2)}) copy-start(bf16[2,64,12,64]{1,3,2,0:T(8,128)(2,1)S(1)} %copy.180) | copy-start | bytes 589828
  118.5 5.3 copy-start.2
  147.3 26.7 %copy-start.25 = (bf16[2,512,768]{1,2,0:T(8,128)(2,1)}, bf16[2,512,768]{1,2,0:T(8,128)(2,1)S(1)}, u32[]{:S(2)}) copy-start(bf16[2,512,768]{1,2,0:T(8,128)(2,1)S(1)} %copy.152) | copy-start | bytes 4718596
  174.0 4.0 copy-start.28
  255.7 118.5 %copy-start.12 = (f32[128,768]{1,0:T(8,128)}, f32[128,768]{1,0:T(8,128)S(1)}, u32[]{:S(2)}) copy-start(f32[128,768]{1,0:T(8,128)S(1)} %get-tuple-element.353) | copy-start | bytes 1179652
  312.6 6.8 copy-start.3
  349.9 79.6 %reduce-scatter.33.cloned.1.call-start = ((), (), s32[]{:S(2)}) async-start(), calls=%async_computation.27 | async-start | bytes 3538944
  370.0 92.5 %reduce-scatter.19.cloned.1.call-start = ((), (), s32[]{:S(2)}) async-start(), calls=%async_computation.20 | async-start | bytes 1474560 | tf_op jit(solution)/shard_map/reduce_scatter | solution.py:416
  372.5 121.4 %reduce-scatter.21.cloned.1.call-start = ((), (), s32[]{:S(2)}) async-start(), calls=%async_computation.21 | async-start | bytes 1474560 | tf_op jit(solution)/shard_map/reduce_scatter | solution.py:416
  374.1 179.9 %reduce-scatter.23.cloned.1.call-start = ((), (), s32[]{:S(2)}) async-start(), calls=%async_computation.22 | async-start | bytes 5898240 | tf_op jit(solution)/shard_map/reduce_scatter | solution.py:428
  377.9 236.0 %reduce-scatter.25.cloned.1.call-start = ((), (), s32[]{:S(2)}) async-start(), calls=%async_computation.23 | async-start | bytes 5898240 | tf_op jit(solution)/shard_map/reduce_scatter | solution.py:428
  382.9 291.0 %reduce-scatter.27.cloned.1.call-start = ((), (), s32[]{:S(2)}) async-start(), calls=%async_computation.24 | async-start | bytes 5898240 | tf_op jit(solution)/shard_map/reduce_scatter | solution.py:434
  388.2 345.7 %reduce-scatter.29.cloned.1.call-start = ((), (), s32[]{:S(2)}) async-start(), calls=%async_computation.25 | async-start | bytes 5898240 | tf_op jit(solution)/shard_map/reduce_scatter | solution.py:434
  393.4 390.6 %reduce-scatter.15.cloned.1.call-start = ((), (), s32[]{:S(2)}) async-start(), calls=%async_computation.18 | async-start | bytes 4423680 | tf_op jit(solution)/shard_map/reduce_scatter | solution.py:407
  396.5 38.0 %copy-start.81 = (bf16[128,768]{0,1:T(8,128)(2,1)}, bf16[128,768]{0,1:T(8,128)(2,1)S(1)}, u32[]{:S(2)}) copy-start(bf16[128,768]{0,1:T(8,128)(2,1)S(1)} %convert_element_type.515) | copy-start | bytes 589828
  438.0 396.3 %reduce-scatter.17.cloned.1.call-start = ((), (), s32[]{:S(2)}) async-start(), calls=%async_computation.19 | async-start | bytes 4423680 | tf_op jit(solution)/shard_map/reduce_scatter | solution.py:407
  446.0 4.0 copy-start.7
  446.1 545.0 %all-reduce.32.cloned.1.call-start = ((), (), s32[]{:S(2)}) async-start(), calls=%async_computation.28 | async-start | bytes 14155776 | tf_op jit(solution)/shard_map/psum | solution.py:444
  448.7 3.8 copy-start.100
  834.3 64.6 %copy-start.11 = (bf16[2,2,64,768]{3,2,1,0:T(8,128)(2,1)S(1)}, bf16[2,2,64,768]{3,2,1,0:T(8,128)(2,1)}, u32[]{:S(2)}) copy-start(bf16[2,2,64,768]{3,2,1,0:T(8,128)(2,1)} %param.16) | copy-start | bytes 1179652
  834.3 64.6 %copy-start.32 = (bf16[1,2,64,768]{3,2,1,0:T(8,128)(2,1)S(1)}, bf16[1,2,64,768]{3,2,1,0:T(8,128)(2,1)}, u32[]{:S(2)}) copy-start(bf16[1,2,64,768]{3,2,1,0:T(8,128)(2,1)} %copy-done.30) | copy-start | bytes 589828
  834.3 64.6 %copy-start.36 = (bf16[1,2,64,768]{3,2,1,0:T(8,128)(2,1)S(1)}, bf16[1,2,64,768]{3,2,1,0:T(8,128)(2,1)}, u32[]{:S(2)}) copy-start(bf16[1,2,64,768]{3,2,1,0:T(8,128)(2,1)} %copy-done.33) | copy-start | bytes 589828
  834.3 64.6 %copy-start.48 = (f32[128,768]{1,0:T(8,128)S(1)}, f32[128,768]{1,0:T(8,128)}, u32[]{:S(2)}) copy-start(f32[128,768]{1,0:T(8,128)} %copy-done.47) | copy-start | bytes 1179652
  834.3 64.6 %copy-start.49 = (f32[128,768]{1,0:T(8,128)S(1)}, f32[128,768]{1,0:T(8,128)}, u32[]{:S(2)}) copy-start(f32[128,768]{1,0:T(8,128)} %get-tuple-element.334) | copy-start | bytes 1179652
  834.3 67.2 %copy-start.13 = (f32[128,768]{1,0:T(8,128)S(1)}, f32[128,768]{1,0:T(8,128)}, u32[]{:S(2)}) copy-start(f32[128,768]{1,0:T(8,128)} %copy-done.12) | copy-start | bytes 1179652
  834.3 67.2 %copy-start.40 = (f32[128,3072]{1,0:T(8,128)S(1)}, f32[128,3072]{1,0:T(8,128)}, u32[]{:S(2)}) copy-start(f32[128,3072]{1,0:T(8,128)} %get-tuple-element.354) | copy-start | bytes 4718596
  899.0 6.1 slice-start
  905.2 4.3 copy-start.131
  905.2 4.3 copy-start.132
  905.2 4.8 copy-start.129
  905.2 4.8 copy-start.130
  905.2 5.4 copy-start.127
  905.3 5.4 copy-start.128
  905.3 5.9 copy-start.125
  905.3 5.9 copy-start.126
  905.3 6.5 copy-start.117
  905.3 6.5 copy-start.118
  (109 other events, 227.6 us)
Sparse Core Ops, SparseCore 0:
  10.0 49.4 all-gather.11
  61.2 57.1 all-gather.21
  120.1 25.4 all-gather.13
  147.6 24.5 all-gather.15
  173.7 24.5 all-gather.23
  200.4 24.5 all-gather.25
  226.8 26.8 all-gather.17
  255.5 57.0 all-gather.19
  350.0 37.8 reduce-scatter.30
  390.0 39.4 reduce-scatter.32
  432.4 30.0 reduce-scatter.18
  465.3 28.5 reduce-scatter.20
  496.8 57.0 reduce-scatter.22
  556.8 57.0 reduce-scatter.24
  616.8 57.0 reduce-scatter.26
  676.8 57.0 reduce-scatter.28
  736.8 47.2 reduce-scatter.14
  787.0 47.2 reduce-scatter.16
  837.3 153.7 all-reduce.31
where the time goes:
time: 1010 us
  waiting for transfers between devices  693 us (69%)
  matrix products  86.4 us (9%)
  blocking collectives  82.9 us (8%)
  local copies, waits for them, and re-layouts  81.8 us (8%)
  other arithmetic  42.3 us (4%)
  between operations  18.2 us (2%)
    reduce_scatter x2, waiting for transfers between devices, per_device(): lax.psum_scatter(local_grads[9].astype(jnp.bfloat16), 'fsdp', scatter_dim...  120 us
    reduce_scatter x2, waiting for transfers between devices, per_device(): lax.psum_scatter(local_grads[11].astype(jnp.bfloat16), 'fsdp', scatter_di...  120 us
    reduce_scatter x2, waiting for transfers between devices, per_device(): lax.psum_scatter(local_grads[2].astype(jnp.bfloat16), 'fsdp', scatter_dim...  100 us
    psum x1, waiting for transfers between devices, per_device(): lax.psum(shard_part[2].astype(jnp.bfloat16), 'ctx').astype(jnp.float32)  78.7 us
    all_gather x1, waiting for transfers between devices, per_device(): lax.all_gather(owned[9], 'fsdp', axis=0, tiled=True)  52.9 us
    unnamed x348, local copies, waits for them, and re-layouts  51.4 us
    all_gather x2, waiting for transfers between devices, per_device(): value_part = lax.all_gather(shipped[1], 'ctx', axis=1, tiled=True)  49 us
    reduce_scatter x2, waiting for transfers between devices, per_device(): lax.psum_scatter(local_grads[5].astype(jnp.bfloat16), 'fsdp', scatter_dim...  37.6 us
  transfers between devices with their start and end apart: 19, of which 18 were waited for; matrix products, arithmetic and copies ran while one was open for 15% of the time, Pallas kernels for 0%

commit v1 on v0

--- a/solution.py
+++ b/solution.py
@@ -1,6 +1,11 @@
+import functools
+import math
+
 import jax
 import jax.numpy as jnp
 from jax import lax
+from jax.experimental import pallas as pl
+from jax.experimental.pallas import tpu as pltpu
 from jax.sharding import PartitionSpec as P
 
 HEADS = 12
@@ -460,6 +465,649 @@
     return (jnp.stack(outputs_list), jnp.stack(input_grads)) + tuple(summed_shards)
 
 
+MESH = pl.DeviceIdType.MESH
+F32 = jnp.float32
+BF16 = jnp.bfloat16
+GELU_A = math.sqrt(2.0 / math.pi)
+GELU_B = 0.044715
+LN1_S, LN1_B, B_Q, B_V, B_P, LN2_S, LN2_B, B_D, B_U = range(9)
+
+
+def dot_nn(left, right):
+    return lax.dot_general(left, right, (((1,), (0,)), ((), ())), preferred_element_type=F32)
+
+
+def dot_nt(left, right):
+    return lax.dot_general(left, right, (((1,), (1,)), ((), ())), preferred_element_type=F32)
+
+
+def dot_tn(left, right):
+    return lax.dot_general(left, right, (((0,), (0,)), ((), ())), preferred_element_type=F32)
+
+
+def mult(value, factor):
+    return pl.multiple_of(value, factor)
+
+
+def loop_rows(total, step, body):
+    def once(turn, carry):
+        body(mult(turn * step, step))
+        return carry
+
+    lax.fori_loop(0, total // step, once, 0)
+
+
+def norm_parts(values):
+    center = values - jnp.mean(values, -1, keepdims=True)
+    spread = jnp.mean(center * center, -1, keepdims=True)
+    inv = lax.rsqrt(spread + NORM_EPS)
+    return center * inv, inv
+
+
+def norm_back(d_out, hat, inv, scale):
+    d_hat = d_out * scale
+    return inv * (
+        d_hat - jnp.mean(d_hat, -1, keepdims=True) - hat * jnp.mean(d_hat * hat, -1, keepdims=True)
+    )
+
+
+def layer_kernel(
+    inp, seg, pv, wq, wp, wu, wd, bu, cot,
+    out_ref, din_ref, gd_ref, gu_ref, gp_ref, gq_ref, sg_ref,
+    X, SEG, COT, H2, PV, WQ, WP, WU, WD, H1, Q, K, V, E, MB, ATT, LI, MIX, RES, ACT, DPRE,
+    PDH, RDH, RDI, PO, RO, ROI, OUTB, DRES, DBR, DBX, DMS, DM, DOS, DLT, DQKV,
+    GD, Z1D, ZSD, Z2D, ZFD, GU, RGU, Z1U, ZSU, Z2U, ZFU, GPP, RGP, GP, Z1P, ZSP, Z2P, ZFP,
+    GQ, RGQ, GQF, Z1Q, ZSQ, Z2Q, ZFQ, PD1, RD1, DIN, SGP, SGS, SGB, SGF, SGZ, GBU,
+    send_sem, recv_sem, local_sem,
+):
+    f = lax.axis_index("fsdp")
+    c = lax.axis_index("ctx")
+    z = c // 2
+    h = c % 2
+    o = 1 - h
+    fpeers = (f + 1 - 2 * (f % 2), (f + 2) % 4, 3 - f)
+    zpeers = (z + 1 - 2 * (z % 2), (z + 2) % 4, 3 - z)
+    sib = (f, 2 * z + o)
+    shard = inp.shape[1]
+    half = 4 * shard
+    rows_all = 2 * half
+    wide = X.shape[1]
+    hw = wide // 2
+    kr = wide // 4
+    own_rows = pl.ds(mult(h * half, half), half)
+    oth_rows = pl.ds(mult(o * half, half), half)
+    my_block = pl.ds(mult(h * half + z * shard, shard), shard)
+    counts = [0, 0]
+
+    def rc_make(src, dst, dev):
+        i = counts[0]
+        counts[0] += 1
+        return pltpu.make_async_remote_copy(
+            src_ref=src, dst_ref=dst, send_sem=send_sem.at[i], recv_sem=recv_sem.at[i],
+            device_id=dev, device_id_type=MESH,
+        )
+
+    sent = []
+
+    def rc(src, dst, dev):
+        copy = rc_make(src, dst, dev)
+        copy.start()
+        sent.append(copy)
+        return copy
+
+    def lc(src, dst):
+        i = counts[1]
+        counts[1] += 1
+        copy = pltpu.make_async_copy(src, dst, local_sem.at[i])
+        copy.start()
+        return copy
+
+    def chunk_rows(j):
+        return pl.ds(mult(j * rows_all + h * half, half), half)
+
+    def chunk_other(j):
+        return pl.ds(mult(j * rows_all + o * half, half), half)
+
+    barrier = pltpu.get_barrier_semaphore()
+    everyone = [(fp, c) for fp in fpeers] + [(f, 2 * zp + h) for zp in zpeers] + [sib]
+    for dev in everyone:
+        pl.semaphore_signal(barrier, inc=1, device_id=dev, device_id_type=MESH)
+    pl.semaphore_wait(barrier, len(everyone))
+
+    def cols(start):
+        return pl.ds(mult(start, 128), hw)
+
+    def krows(j):
+        return pl.ds(mult(j * kr, kr), kr)
+
+    x_in = [rc(inp.at[zp], X.at[my_block], (f, 2 * zp + h)) for zp in zpeers]
+    s_in = [rc(seg.at[zp], SEG.at[my_block], (f, 2 * zp + h)) for zp in zpeers]
+    pv_in = [rc(pv, PV.at[f], (fp, c)) for fp in fpeers]
+    wq_in = [
+        rc(wq.at[:, cols(b * wide + h * hw)], WQ.at[b, krows(f)], (fp, c))
+        for b in range(3)
+        for fp in fpeers
+    ]
+    cot_block = pl.ds(mult(f * rows_all + h * half + z * shard, shard), shard)
+    c_in = [rc(cot.at[zp], COT.at[cot_block], (f, 2 * zp + h)) for zp in zpeers]
+    x_own = lc(inp.at[z], X.at[my_block])
+    s_own = lc(seg.at[z], SEG.at[my_block])
+    pv_own = lc(pv, PV.at[f])
+    wq_own = [lc(wq.at[:, cols(b * wide + h * hw)], WQ.at[b, krows(f)]) for b in range(3)]
+    c_own = lc(cot.at[z], COT.at[cot_block])
+    wd_own = lc(wd.at[pl.ds(mult(h * hw, hw), hw)], WD)
+    wu_own = lc(wu.at[:, cols(f * wide + h * hw)], WU.at[krows(f)])
+    wp_own = lc(wp.at[:, cols(h * hw)], WP.at[h, krows(f)])
+
+    x_own.wait()
+    s_own.wait()
+    for copy in x_in + s_in:
+        copy.wait_recv()
+    x_sib = rc(X.at[own_rows], X.at[own_rows], sib)
+    s_sib = rc(SEG.at[own_rows], SEG.at[own_rows], sib)
+    pv_own.wait()
+    for copy in pv_in:
+        copy.wait_recv()
+    vec = PV[0] + PV[1] + PV[2] + PV[3]
+    PV[0] = vec
+
+    def vector(i):
+        return PV[0, i : i + 1, :]
+
+    SGP[...] = jnp.zeros_like(SGP)
+    GBU[...] = jnp.zeros_like(GBU)
+    x_sib.wait_recv()
+    s_sib.wait_recv()
+
+    def ln1(r):
+        hat, _ = norm_parts(X[pl.ds(r, 64), :].astype(F32))
+        H1[pl.ds(r, 64), :] = (hat * vector(LN1_S) + vector(LN1_B)).astype(BF16)
+
+    loop_rows(rows_all, 64, ln1)
+    seg_row = jnp.transpose(SEG[...])[0:1, :]
+
+    def mask(r):
+        seg_col = SEG[pl.ds(r, 128), 0:1]
+        place_q = r + lax.broadcasted_iota(jnp.int32, (128, rows_all), 0)
+        place_k = lax.broadcasted_iota(jnp.int32, (128, rows_all), 1)
+        allowed = (seg_col == seg_row) & ((seg_row >= 0.0) | (place_q == place_k))
+        MB[pl.ds(r, 128), :] = jnp.where(allowed, 0.0, MASKED)
+
+    loop_rows(rows_all, 128, mask)
+    c_own.wait()
+    for copy in c_in:
+        copy.wait_recv()
+    c_sib = rc(COT.at[chunk_rows(f)], COT.at[chunk_rows(f)], sib)
+
+    for copy in wq_own:
+        copy.wait()
+    for copy in wq_in:
+        copy.wait_recv()
+    wp_own.wait()
+    wp_in = [rc(wp.at[:, cols(h * hw)], WP.at[h, krows(f)], (fp, c)) for fp in fpeers]
+    wu_in = [rc(wu.at[:, cols(fp * wide + h * hw)], WU.at[krows(f)], (fp, c)) for fp in fpeers]
+    cot_in = [rc(COT.at[chunk_rows(f)], COT.at[chunk_rows(f)], (fp, c)) for fp in fpeers]
+    bias_half = [PV[0, i : i + 1, cols(h * hw)] for i in (B_Q, B_V)]
+    pairs = hw // 128
+    for b, target in ((0, Q), (1, K), (2, V)):
+        prod = dot_nn(H1[...], WQ[b])
+        if b == 0:
+            prod = (prod + bias_half[0]).astype(BF16) * SCORE_SCALE
+        if b == 2:
+            prod = prod + bias_half[1]
+        prod = prod.astype(BF16)
+        for p in range(pairs):
+            target[p] = prod[:, p * 128 : (p + 1) * 128]
+
+    lane = lax.broadcasted_iota(jnp.int32, (1, 128), 1)
+    low_half = lane < 64
+
+    def pick(s, values):
+        keep = low_half if s == 0 else jnp.logical_not(low_half)
+        return jnp.where(keep, values, jnp.zeros_like(values))
+
+    mix_out = []
+    for p in range(pairs):
+
+        def attend(r, p=p):
+            rows = pl.ds(r, 128)
+            total = None
+            for s in range(2):
+                scores = dot_nt(pick(s, Q[p, rows, :]), K[p]) + MB[rows, :]
+                top = jnp.max(scores, -1, keepdims=True)
+                expo = jnp.exp(scores - top)
+                inv = 1.0 / jnp.sum(expo, -1, keepdims=True)
+                low = expo.astype(BF16)
+                E[2 * p + s, rows, :] = low
+                LI[2 * p + s, rows, :] = inv
+                part = dot_nn(low, pick(s, V[p])) * inv
+                total = part if total is None else total + part
+            ATT[p, rows, :] = total
+            MIX[3 * h + p, rows, :] = total.astype(BF16)
+
+        loop_rows(rows_all, 128, attend)
+        mix_out.append(rc(MIX.at[3 * h + p], MIX.at[3 * h + p], sib))
+
+    for copy in wp_in:
+        copy.wait_recv()
+    wp_sib = rc(WP.at[h], WP.at[h], sib)
+    for copy in mix_out:
+        copy.wait_recv()
+    wp_sib.wait_recv()
+
+    def project(r):
+        rows = pl.ds(mult(h * half + r, 64), 64)
+        mixed = jnp.concatenate([MIX[g, rows, :] for g in range(2 * pairs)], axis=1)
+        branch = jnp.concatenate([dot_nn(mixed, WP[k]) for k in range(2)], axis=1)
+        resid = X[rows, :].astype(F32) + branch + vector(B_P)
+        RES[pl.ds(r, 64), :] = resid
+        hat, _ = norm_parts(resid)
+        H2[pl.ds(mult(f * rows_all + h * half + r, 64), 64), :] = (
+            hat * vector(LN2_S) + vector(LN2_B)
+        ).astype(BF16)
+
+    loop_rows(half, 64, project)
+    h2_in = [rc(H2.at[chunk_rows(f)], H2.at[chunk_rows(f)], (fp, c)) for fp in fpeers]
+    h2_sib = rc(H2.at[chunk_rows(f)], H2.at[chunk_rows(f)], sib)
+
+    for copy in wu_in:
+        copy.wait_recv()
+    wu_own.wait()
+    wd_own.wait()
+    c_sib.wait_recv()
+    h2_sib.wait_recv()
+    bias_up = bu[h]
+
+    def mlp(j):
+        def block(r):
+            rows = pl.ds(mult(j * rows_all + r, 128), 128)
+            pre = dot_nn(H2[rows, :], WU[...]) + bias_up
+            square = pre * pre
+            tan = jnp.tanh(GELU_A * pre * (1.0 + GELU_B * square))
+            low = (0.5 * pre * (1.0 + tan)).astype(BF16)
+            slope = 0.5 * (1.0 + tan) + (0.5 * GELU_A) * pre * (1.0 - tan * tan) * (
+                1.0 + (3.0 * GELU_B) * square
+            )
+            ACT[rows, :] = low
+            d_pre = (dot_nt(COT[rows, :], WD[...]) * slope).astype(BF16)
+            DPRE[rows, :] = d_pre
+            GBU[...] += jnp.sum(d_pre.astype(F32), 0, keepdims=True)
+            PDH[rows, :] = dot_nt(d_pre, WU[...]).astype(BF16)
+            PO[rows, :] = dot_nn(low, WD[...]).astype(BF16)
+
+        loop_rows(rows_all, 128, block)
+        first = rc(PDH.at[chunk_other(j)], RDH.at[j], sib)
+        second = rc(PO.at[chunk_other(j)], RO.at[j], sib)
+        return first, second
+
+    def join(buf, got, j):
+        def block(r):
+            rows = pl.ds(mult(j * rows_all + h * half + r, 64), 64)
+            buf[rows, :] = (buf[rows, :].astype(F32) + got[j, pl.ds(r, 64), :].astype(F32)).astype(BF16)
+
+        loop_rows(half, 64, block)
+
+    own_pair = mlp(f)
+    fwd = []
+    for i, fp in enumerate(fpeers):
+        cot_in[i].wait_recv()
+        fwd.append(rc(COT.at[chunk_rows(fp)], COT.at[chunk_rows(fp)], sib))
+    h2_fwd = []
+    for i in range(2):
+        h2_in[i].wait_recv()
+        h2_fwd.append(rc(H2.at[chunk_rows(fpeers[i])], H2.at[chunk_rows(fpeers[i])], sib))
+    pairs_out = []
+    dh_in = []
+    for i, fp in enumerate(fpeers):
+        fwd[i].wait_recv()
+        h2_fwd[i].wait_recv()
+        pairs_out.append(mlp(fp))
+        if i == 0:
+            h2_in[2].wait_recv()
+            h2_fwd.append(rc(H2.at[chunk_rows(fpeers[2])], H2.at[chunk_rows(fpeers[2])], sib))
+        pairs_out[i][0].wait_recv()
+        join(PDH, RDH, fp)
+        dh_in.append(rc(PDH.at[chunk_rows(fp)], RDI.at[f], (fp, c)))
+    o_in = []
+    for i, fp in enumerate(fpeers):
+        pairs_out[i][1].wait_recv()
+        join(PO, RO, fp)
+        o_in.append(rc(PO.at[chunk_rows(fp)], ROI.at[f], (fp, c)))
+
+    inner = (z + 1) // 2 == 1
+    outer = jnp.logical_not(inner)
+    toward = (f, 2 * zpeers[0] + h)
+    across = (f, 2 * zpeers[2] + h)
+
+    class Chain:
+        def __init__(self, own, z1, zs, z2, zf):
+            self.own, self.z1, self.zs, self.z2, self.zf = own, z1, zs, z2, zf
+            self.c1 = rc_make(own, z1, toward)
+            self.c2 = rc_make(zs, z2, across)
+            self.c3 = rc_make(zf.at[h], zf.at[h], toward)
+            self.c4 = rc_make(zf.at[h], zf.at[h], sib)
+
+        def first(self):
+            @pl.when(outer)
+            def _():
+                self.c1.start()
+
+        def second(self):
+            @pl.when(inner)
+            def _():
+                self.c1.wait_recv()
+                self.zs[...] = (self.own[...].astype(F32) + self.z1[...].astype(F32)).astype(BF16)
+                self.c2.start()
+
+        def third(self):
+            @pl.when(inner)
+            def _():
+                self.c2.wait_recv()
+                self.zf[h] = (self.zs[...].astype(F32) + self.z2[...].astype(F32)).astype(BF16)
+                self.c3.start()
+
+        def fourth(self):
+            @pl.when(outer)
+            def _():
+                self.c3.wait_recv()
+                self.c1.wait_send()
+
+            @pl.when(inner)
+            def _():
+                self.c2.wait_send()
+                self.c3.wait_send()
+
+            self.c4.start()
+
+        def fifth(self):
+            self.c4.wait_recv()
+            self.c4.wait_send()
+
+    GD[...] = dot_tn(ACT[...], COT[...]).astype(BF16)
+    chain_d = Chain(GD, Z1D, ZSD, Z2D, ZFD)
+    chain_d.first()
+    GU[...] = dot_tn(H2[...], DPRE[...]).astype(BF16)
+    gu_in = [rc(GU.at[krows(fp)], RGU.at[f], (fp, c)) for fp in fpeers]
+    RGU[f] = GU[krows(f), :]
+    SGP[B_U : B_U + 1, cols(h * hw)] = GBU[...]
+
+    own_pair[0].wait_recv()
+    for copy in dh_in:
+        copy.wait_recv()
+
+    def ln2_back(r):
+        rows = pl.ds(r, 64)
+        mine = pl.ds(mult(f * rows_all + h * half + r, 64), 64)
+        d_h2 = PDH[mine, :].astype(F32) + RDH[f, rows, :].astype(F32)
+        for fp in fpeers:
+            d_h2 = d_h2 + RDI[fp, rows, :].astype(F32)
+        hat, inv = norm_parts(RES[rows, :])
+        SGP[LN2_S : LN2_S + 1, :] += jnp.sum(d_h2 * hat, 0, keepdims=True)
+        SGP[LN2_B : LN2_B + 1, :] += jnp.sum(d_h2, 0, keepdims=True)
+        cot_rows = COT[mine, :].astype(F32)
+        SGP[B_D : B_D + 1, :] += jnp.sum(cot_rows, 0, keepdims=True)
+        d_resid = cot_rows + norm_back(d_h2, hat, inv, vector(LN2_S))
+        DRES[rows, :] = d_resid
+        low = d_resid.astype(BF16)
+        SGP[B_P : B_P + 1, :] += jnp.sum(low.astype(F32), 0, keepdims=True)
+        for k in range(2):
+            DBR[k, rows, :] = low[:, k * hw : (k + 1) * hw]
+        d_mixed = dot_nt(low[:, :hw], WP[0]) + dot_nt(low[:, hw:], WP[1])
+        d_mixed = d_mixed.astype(BF16)
+        for g in range(2 * pairs):
+            DMS[g, rows, :] = d_mixed[:, g * 128 : (g + 1) * 128]
+
+    loop_rows(half, 64, ln2_back)
+    dm_sib = rc(DMS.at[pl.ds(3 * o, 3)], DM.at[:, own_rows, :], sib)
+    dbr_sib = rc(DBR.at[o], DBX.at[own_rows], sib)
+    DM[:, own_rows, :] = DMS[pl.ds(3 * h, 3)]
+    DBX[own_rows, :] = DBR[h]
+    chain_d.second()
+    dbr_sib.wait_recv()
+    mixed_all = jnp.concatenate([MIX[g] for g in range(2 * pairs)], axis=1)
+    GPP[...] = dot_tn(mixed_all, DBX[...]).astype(BF16)
+    gp_in = [rc(GPP.at[krows(fp)], RGP.at[f], (fp, c)) for fp in fpeers]
+    dm_sib.wait_recv()
+
+    def attention_back(p):
+        def prepare(r):
+            rows = pl.ds(r, 128)
+            d_out = DM[p, rows, :].astype(F32)
+            for s in range(2):
+                scaled = pick(s, d_out * LI[2 * p + s, rows, :]).astype(BF16)
+                DOS[s, rows, :] = scaled
+                DLT[s, rows, :] = jnp.sum(scaled.astype(F32) * ATT[p, rows, :], -1, keepdims=True)
+
+        loop_rows(rows_all, 128, prepare)
+        here = slice(p * 128, (p + 1) * 128)
+        d_value = dot_tn(E[2 * p], DOS[0]) + dot_tn(E[2 * p + 1], DOS[1])
+        DQKV[2, :, here] = d_value.astype(BF16)
+
+        def block(r):
+            rows = pl.ds(r, 128)
+            d_query = None
+            for s in range(2):
+                d_probs = dot_nt(DOS[s, rows, :], V[p])
+                d_scores = (
+                    E[2 * p + s, rows, :].astype(F32) * (d_probs - DLT[s, rows, :])
+                ).astype(BF16)
+                E[2 * p + s, rows, :] = d_scores
+                part = dot_nn(d_scores, pick(s, K[p]))
+                d_query = part if d_query is None else d_query + part
+            DQKV[0, rows, here] = (d_query * SCORE_SCALE).astype(BF16)
+
+        loop_rows(rows_all, 128, block)
+        d_key = dot_tn(E[2 * p], pick(0, Q[p])) + dot_tn(E[2 * p + 1], pick(1, Q[p]))
+        DQKV[1, :, here] = d_key.astype(BF16)
+
+    attention_back(0)
+    chain_d.third()
+    for copy in gu_in:
+        copy.wait_recv()
+    chain_u = Chain(RGU, Z1U, ZSU, Z2U, ZFU)
+    chain_u.first()
+    attention_back(1)
+    chain_d.fourth()
+    own_pair[1].wait_recv()
+    for copy in o_in:
+        copy.wait_recv()
+
+    def finish(r):
+        rows = pl.ds(r, 64)
+        mine = pl.ds(mult(f * rows_all + h * half + r, 64), 64)
+        total = PO[mine, :].astype(F32) + RO[f, rows, :].astype(F32)
+        for fp in fpeers:
+            total = total + ROI[fp, rows, :].astype(F32)
+        OUTB[rows, :] = (RES[rows, :] + total + vector(B_D)).astype(BF16)
+
+    loop_rows(half, 64, finish)
+
+    def block_of(zp):
+        return pl.ds(mult(zp * shard, shard), shard)
+
+    res_in = [rc(OUTB.at[block_of(zp)], out_ref.at[z], (f, 2 * zp + h)) for zp in zpeers]
+    res_own = lc(OUTB.at[block_of(z)], out_ref.at[z])
+    chain_u.second()
+    for copy in gp_in:
+        copy.wait_recv()
+
+    def owned_sum(own, got):
+        total = own.astype(F32)
+        for fp in fpeers:
+            total = total + got[fp].astype(F32)
+        return total.astype(BF16)
+
+    GP[...] = owned_sum(GPP[krows(f), :], RGP)
+    chain_p = Chain(GP, Z1P, ZSP, Z2P, ZFP)
+    chain_p.first()
+    attention_back(2)
+    chain_u.third()
+    chain_p.second()
+
+    for b in range(3):
+        GQ[b] = dot_tn(H1[...], DQKV[b]).astype(BF16)
+    gq_in = [rc(GQ.at[:, krows(fp), :], RGQ.at[f], (fp, c)) for fp in fpeers]
+    PD1[...] = (
+        dot_nt(DQKV[0], WQ[0]) + dot_nt(DQKV[1], WQ[1]) + dot_nt(DQKV[2], WQ[2])
+    ).astype(BF16)
+    d1_sib = rc(PD1.at[oth_rows], RD1, sib)
+    for b, i in ((0, B_Q), (2, B_V)):
+        SGP[i : i + 1, cols(h * hw)] = jnp.sum(DQKV[b].astype(F32), 0, keepdims=True)
+    d1_sib.wait_recv()
+
+    def ln1_back(r):
+        rows = pl.ds(r, 64)
+        mine = pl.ds(mult(h * half + r, 64), 64)
+        d_h1 = PD1[mine, :].astype(F32) + RD1[rows, :].astype(F32)
+        hat, inv = norm_parts(X[mine, :].astype(F32))
+        SGP[LN1_S : LN1_S + 1, :] += jnp.sum(d_h1 * hat, 0, keepdims=True)
+        SGP[LN1_B : LN1_B + 1, :] += jnp.sum(d_h1, 0, keepdims=True)
+        DIN[rows, :] = (DRES[rows, :] + norm_back(d_h1, hat, inv, vector(LN1_S))).astype(BF16)
+
+    loop_rows(half, 64, ln1_back)
+    din_in = [rc(DIN.at[block_of(zp)], din_ref.at[z], (f, 2 * zp + h)) for zp in zpeers]
+    din_own = lc(DIN.at[block_of(z)], din_ref.at[z])
+    sg_sib = rc(SGP, SGS, sib)
+    chain_u.fourth()
+    chain_p.third()
+    chain_p.fourth()
+    sg_sib.wait_recv()
+    SGB[f] = SGP[...] + SGS[...]
+    sgf_in = [rc(SGB.at[f], SGB.at[f], (fp, c)) for fp in fpeers]
+
+    for copy in gq_in:
+        copy.wait_recv()
+    for b in range(3):
+        total = GQ[b, krows(f), :].astype(F32)
+        for fp in fpeers:
+            total = total + RGQ[fp, b].astype(F32)
+        GQF[b] = total.astype(BF16)
+    chain_q = Chain(GQF, Z1Q, ZSQ, Z2Q, ZFQ)
+    chain_q.first()
+    for copy in sgf_in:
+        copy.wait_recv()
+    plane = SGB[0] + SGB[1] + SGB[2] + SGB[3]
+    row_id = lax.broadcasted_iota(jnp.int32, plane.shape, 0)
+    SGZ[z] = jnp.where(row_id == B_U, SGB[f], plane)
+    sgz_in = [rc(SGZ.at[z], SGZ.at[z], (f, 2 * zp + h)) for zp in zpeers]
+    chain_q.second()
+    chain_d.fifth()
+    outs = [lc(ZFD.at[k], gd_ref.at[pl.ds(k * hw, hw)]) for k in range(2)]
+    chain_u.fifth()
+    outs += [
+        lc(ZFU.at[k, s], gu_ref.at[:, pl.ds(s * wide + k * hw, hw)]) for k in range(2) for s in range(4)
+    ]
+    chain_p.fifth()
+    outs += [lc(ZFP.at[k], gp_ref.at[:, pl.ds(k * hw, hw)]) for k in range(2)]
+    chain_q.third()
+    for copy in sgz_in:
+        copy.wait_recv()
+    sg_ref[...] = SGZ[0] + SGZ[1] + SGZ[2] + SGZ[3]
+    chain_q.fourth()
+    chain_q.fifth()
+    outs += [
+        lc(ZFQ.at[k, b], gq_ref.at[:, pl.ds(b * wide + k * hw, hw)]) for k in range(2) for b in range(3)
+    ]
+    for copy in res_in + din_in:
+        copy.wait_recv()
+    for copy in outs + [res_own, din_own]:
+        copy.wait()
+    for copy in sent:
+        copy.wait_send()
+
+
+def fast_device(
+    inputs, segments, ln1_scale, ln1_bias, w_qkv, b_query, b_value, w_proj, b_proj,
+    ln2_scale, ln2_bias, w_up, b_up, w_down, b_down, cotangent,
+):
+    micro_count, seq_dev, shard, wide = inputs.shape
+    seqs = micro_count * seq_dev
+    rows_all = 8 * shard
+    half = rows_all // 2
+    hw = wide // 2
+    kr = wide // 4
+    pairs = hw // 128
+    heads = 2 * pairs
+    f = lax.axis_index("fsdp")
+    vectors = jnp.stack(
+        (ln1_scale, ln1_bias, b_query, b_value, b_proj, ln2_scale, ln2_bias, b_down)
+    ).astype(F32)
+    spot = lax.broadcasted_iota(jnp.int32, (8, wide), 1) // kr == f
+    packed = jnp.where(spot, jnp.tile(vectors, (1, 4)), 0.0)
+    seg_wide = jnp.broadcast_to(
+        segments.reshape(seqs, shard, 1).astype(F32), (seqs, shard, 128)
+    )
+
+    def vm(*shape, dtype=BF16):
+        return pltpu.VMEM(shape, dtype)
+
+    f32 = functools.partial(vm, dtype=F32)
+    scratch = [
+        vm(rows_all, wide), f32(rows_all, 128), vm(4 * rows_all, wide), vm(4 * rows_all, wide),
+        f32(4, 8, wide), vm(3, wide, hw), vm(2, wide, hw), vm(wide, hw), vm(hw, wide),
+        vm(rows_all, wide), vm(pairs, rows_all, 128), vm(pairs, rows_all, 128),
+        vm(pairs, rows_all, 128), vm(heads, rows_all, rows_all), f32(rows_all, rows_all),
+        f32(pairs, rows_all, 128), f32(heads, rows_all, 1), vm(2 * pairs, rows_all, 128),
+        f32(half, wide), vm(4 * rows_all, hw), vm(4 * rows_all, hw),
+        vm(4 * rows_all, wide), vm(4, half, wide), vm(4, half, wide),
+        vm(4 * rows_all, wide), vm(4, half, wide), vm(4, half, wide), vm(half, wide),
+        f32(half, wide), vm(2, half, hw), vm(rows_all, hw), vm(2 * pairs, half, 128),
+        vm(pairs, rows_all, 128), vm(2, rows_all, 128), f32(2, rows_all, 1),
+        vm(3, rows_all, hw),
+        vm(hw, wide), vm(hw, wide), vm(hw, wide), vm(hw, wide), vm(2, hw, wide),
+        vm(wide, hw), vm(4, kr, hw), vm(4, kr, hw), vm(4, kr, hw), vm(4, kr, hw), vm(2, 4, kr, hw),
+        vm(wide, hw), vm(4, kr, hw), vm(kr, hw), vm(kr, hw), vm(kr, hw), vm(kr, hw), vm(2, kr, hw),
+        vm(3, wide, hw), vm(4, 3, kr, hw), vm(3, kr, hw), vm(3, kr, hw), vm(3, kr, hw),
+        vm(3, kr, hw), vm(2, 3, kr, hw),
+        vm(rows_all, wide), vm(half, wide), vm(half, wide),
+        f32(16, wide), f32(16, wide), f32(4, 16, wide), f32(16, wide), f32(4, 16, wide), f32(1, hw),
+        pltpu.SemaphoreType.DMA((112,)), pltpu.SemaphoreType.DMA((112,)),
+        pltpu.SemaphoreType.DMA((40,)),
+    ]
+    hbm = pl.BlockSpec(memory_space=pl.ANY)
+    vmem = pl.BlockSpec(memory_space=pltpu.VMEM)
+    tokens = jax.ShapeDtypeStruct((seqs, shard, wide), BF16)
+    results = pl.pallas_call(
+        layer_kernel,
+        out_shape=(
+            tokens, tokens,
+            jax.ShapeDtypeStruct(w_down.shape, BF16), jax.ShapeDtypeStruct(w_up.shape, BF16),
+            jax.ShapeDtypeStruct(w_proj.shape, BF16), jax.ShapeDtypeStruct(w_qkv.shape, BF16),
+            jax.ShapeDtypeStruct((16, wide), F32),
+        ),
+        in_specs=[hbm] * 7 + [vmem, hbm],
+        out_specs=(hbm,) * 6 + (vmem,),
+        scratch_shapes=scratch,
+        compiler_params=pltpu.CompilerParams(
+            collective_id=0, has_side_effects=True, vmem_limit_bytes=62 << 20
+        ),
+    )(
+        inputs.reshape(tokens.shape), seg_wide, packed, w_qkv, w_proj, w_up, w_down,
+        b_up.astype(F32).reshape(2, 1, hw), cotangent.reshape(tokens.shape),
+    )
+    out, d_input, g_down, g_up, g_proj, g_qkv, small = results
+    mine = lax.dynamic_slice_in_dim(small[:8], f * kr, kr, 1)
+    return (
+        out.reshape(inputs.shape), d_input.reshape(inputs.shape),
+        mine[LN1_S], mine[LN1_B], g_qkv.astype(F32), mine[B_Q], mine[B_V],
+        g_proj.astype(F32), mine[B_P], mine[LN2_S], mine[LN2_B],
+        g_up.astype(F32), small[B_U], g_down.astype(F32), mine[B_D],
+    )
+
+
+def fits_fast(mesh, inputs, w_up):
+    micro_count, seqs, length, wide = inputs.shape
+    return (
+        mesh.shape["fsdp"] == 4
+        and mesh.shape["ctx"] == 8
+        and micro_count * (seqs // 4) == 4
+        and length == 512
+        and wide == 768
+        and w_up.shape == (wide, 4 * wide)
+        and HEADS * 64 == wide
+    )
+
+
 def solution(mesh):
     placed = (
         P(None, "fsdp", "ctx", None),
@@ -479,8 +1127,12 @@
         P("fsdp"),
         P(None, "fsdp", "ctx", None),
     )
-    return jax.shard_map(
-        per_device,
+    def layer(*args):
+        chosen = fast_device if fits_fast(mesh, args[0], args[11]) else per_device
+        return spread(chosen)(*args)
+
+    spread = functools.partial(
+        jax.shard_map,
         mesh=mesh,
         in_specs=placed,
         out_specs=(
@@ -502,3 +1154,4 @@
         ),
         check_vma=False,
     )
+    return layer

time: 1010 us -> 246 us (0.24)
  waiting for transfers between devices: 693 us -> 0 us
  Pallas kernels: 0 us -> 221 us
  matrix products: 86.4 us -> 0 us
  blocking collectives: 82.9 us -> 0 us
  local copies, waits for them, and re-layouts: 81.8 us -> 11.7 us
  other arithmetic: 42.3 us -> 8.1 us
  between operations: 18.2 us -> 0.68 us
    reduce_scatter x8 -> x0, waiting for transfers between devices: 378 us -> none  [the longest x2 120 us: per_device(): lax.psum_scatter(local_grads[9].astype(jnp.bfloat16), 'fsdp', scatter_dim...]
    pallas_call x0 -> x1, Pallas kernels: none -> 221 us  [fast_device(): pl.pallas_call(layer_kernel, out_shape=(tokens, tokens, jax.ShapeDtypeStr...]
    all_gather x8 -> x0, waiting for transfers between devices: 202 us -> none  [the longest x1 52.9 us: per_device(): lax.all_gather(owned[9], 'fsdp', axis=0, tiled=True)]
    dot_general x36 -> x0, matrix products: 86.4 us -> none  [the longest x8 23.7 us: contract_rows(): lax.dot_general(left, right, (((0,), (0,)), ((), ())), preferred_element_...]
    psum x1 -> x0, waiting for transfers between devices: 78.7 us -> none  [per_device(): lax.psum(shard_part[2].astype(jnp.bfloat16), 'ctx').astype(jnp.float32)]
    unnamed x348 -> x12, local copies, waits for them, and re-layouts: 51.4 us -> 1.51 us
    unnamed x21 -> x0, waiting for transfers between devices: 34.6 us -> none
    all_gather x3 -> x0, blocking collectives: 28 us -> none  [the longest x2 20.8 us: per_device(): seg_part = lax.all_gather(shipped[2], 'ctx', axis=1, tiled=True)]
  transfers between devices with their start and end apart: 19 -> 0, of which waited for: 18 -> 0; matrix products, arithmetic and copies ran while one was open for 15% -> 0% of each run, Pallas kernels for 0% -> 0%
where the time goes in v1:
time: 246 us; the launch traced here: 242 us
  Pallas kernels  221 us (90%)
  local copies, waits for them, and re-layouts  11.7 us (5%)
  other arithmetic  8.1 us (3%)
    pallas_call x1, Pallas kernels, fast_device(): pl.pallas_call(layer_kernel, out_shape=(tokens, tokens, jax.ShapeDtypeStr...  221 us
    another operation x9, local copies, waits for them, and re-layouts, fast_device(): jnp.stack((ln1_scale, ln1_bias, b_query, b_value, b_proj, ln2_scale, ln2_...  5.3 us

profile of v1, /device:TPU:1, one launch (start us, length us, event | category | flops | bytes accessed | tf_op | source)
XLA Modules:
  0.0 241.6 jit_solution(6144525816322181182)
XLA Ops:
  0.7 0.7 stack.27
  1.3 0.7 stack.28
  2.0 0.7 stack.29
  2.6 0.7 stack.30
  3.3 0.7 stack.31
  4.0 0.7 stack.32
  4.6 0.7 stack.33
  5.3 0.7 stack.34
  6.0 0.1 tile.10
  6.1 0.6 fusion.pv
  6.7 0.7 convert_element_type.31
  7.4 0.8 broadcast_in_dim.9.seg
  8.1 1.3 reshape.131.bu
  9.4 221.1 %shard_map.271 = (bf16[4,64,768]{2,1,0:T(8,128)(2,1)}, bf16[4,64,768]{2,1,0:T(8,128)(2,1)}, bf16[768,768]{1,0:T(8,128)(2,1)}, bf16[192,3072]{1,0:T(8,128)(2,1)},...) custom-call(bf16[4,64,768]{2,1,0:T(8,128)(2,1)} %bitcast.13, ...), custom_call_target="tpu_custom_call" | custom-call | tf_op jit(solution)/shard_map/pallas_call | solution.py:1070
  230.5 0.7 slice.30
  231.2 0.7 fusion.4
  231.9 1.3 slice_reduce_fusion
  233.3 0.0 copy-start
  233.3 3.0 %convert_element_type.36 = f32[192,3072]{1,0:T(8,128)} convert(bf16[192,3072]{1,0:T(8,128)(2,1)} %get-tuple-element.27) | non-fusion elementwise | flops 589824 | bytes 3538944 | tf_op jit(solution)/shard_map/convert_element_type | solution.py:1094
  236.3 0.0 copy-done
  236.3 0.0 copy-start.1
  236.3 1.6 convert_element_type.37
  237.9 0.0 copy-done.1
  237.9 0.0 copy-start.4
  237.9 0.0 copy-start.3
  237.9 1.3 convert_element_type.34
  239.2 0.0 copy-start.2
  239.2 0.0 copy-done.4
  239.2 0.9 convert_element_type.35
  240.1 0.0 copy-done.3
  240.1 0.7 copy.33
  240.8 0.0 copy-done.2
  240.8 0.7 copy.34
  (4 shorter events, 0.1 us)
Async XLA Ops:
  233.3 3.0 %copy-start = (bf16[768,768]{1,0:T(8,128)(2,1)S(1)}, bf16[768,768]{1,0:T(8,128)(2,1)}, u32[]{:S(2)}) copy-start(bf16[768,768]{1,0:T(8,128)(2,1)} %get-tuple-element.28) | copy-start | bytes 3538948
  236.3 1.6 copy-start.1
  237.9 1.3 copy-start.4
  237.9 2.2 copy-start.3
  239.2 1.6 copy-start.2

commit v2 on v1

--- a/solution.py
+++ b/solution.py
@@ -512,12 +512,12 @@
 
 
 def layer_kernel(
-    inp, seg, pv, wq, wp, wu, wd, bu, cot,
+    inp, seg, v0, v1, v2, v3, v4, v5, v6, v7, wq, wp, wu, wd, bu, cot,
     out_ref, din_ref, gd_ref, gu_ref, gp_ref, gq_ref, sg_ref,
-    X, SEG, COT, H2, PV, WQ, WP, WU, WD, H1, Q, K, V, E, MB, ATT, LI, MIX, RES, ACT, DPRE,
-    PDH, RDH, RDI, PO, RO, ROI, OUTB, DRES, DBR, DBX, DMS, DM, DOS, DLT, DQKV,
-    GD, Z1D, ZSD, Z2D, ZFD, GU, RGU, Z1U, ZSU, Z2U, ZFU, GPP, RGP, GP, Z1P, ZSP, Z2P, ZFP,
-    GQ, RGQ, GQF, Z1Q, ZSQ, Z2Q, ZFQ, PD1, RD1, DIN, SGP, SGS, SGB, SGF, SGZ, GBU,
+    X, SEGS, SEGR, SEG, COT, H2, PV, VEC, WQ, WP, WU, WD, H1, Q, K, V, E, MB, ATT, LI, MIX, RES,
+    ACT, DPRE, PDH, RDH, RDI, PO, RO, ROI, OUTB, DRES, DBR, DBX, DMS, DM, DOS, DLT, DQKV,
+    GD, Z1D, ZSD, Z2D, ZFD, GU, Z1U, ZSU, Z2U, GUZ, ZFU, GPP, RGP, GP, Z1P, ZSP, Z2P, ZFP,
+    GQ, RGQ, GQF, Z1Q, ZSQ, Z2Q, ZFQ, PD1, RD1, DIN, SGP, SGS, SGB, SGZ, GBU,
     send_sem, recv_sem, local_sem,
 ):
     f = lax.axis_index("fsdp")
@@ -525,15 +525,17 @@
     z = c // 2
     h = c % 2
     o = 1 - h
-    fpeers = (f + 1 - 2 * (f % 2), (f + 2) % 4, 3 - f)
+    fx, fy, fd = fpeers = (f + 1 - 2 * (f % 2), (f + 2) % 4, 3 - f)
     zpeers = (z + 1 - 2 * (z % 2), (z + 2) % 4, 3 - z)
     sib = (f, 2 * z + o)
+    seq_dev = seg.shape[1]
     shard = inp.shape[1]
     half = 4 * shard
     rows_all = 2 * half
     wide = X.shape[1]
     hw = wide // 2
     kr = wide // 4
+    pairs = hw // 128
     own_rows = pl.ds(mult(h * half, half), half)
     oth_rows = pl.ds(mult(o * half, half), half)
     my_block = pl.ds(mult(h * half + z * shard, shard), shard)
@@ -568,87 +570,210 @@
     def chunk_other(j):
         return pl.ds(mult(j * rows_all + o * half, half), half)
 
+    def cols(start):
+        return pl.ds(mult(start, 128), hw)
+
+    def krows(j):
+        return pl.ds(mult(j * kr, kr), kr)
+
+    def hrows(j, i):
+        return pl.ds(mult(j * kr + i * (kr // 2), kr // 2), kr // 2)
+
+    def token_rows(j, i):
+        return pl.ds(mult(j * rows_all + h * half + i * (half // 2), half // 2), half // 2)
+
+    def block_of(zp):
+        return pl.ds(mult(zp * shard, shard), shard)
+
+    class Gather:
+        def __init__(self, own, at):
+            self.at = at
+            self.to_x, self.to_y = {}, {}
+            for first, second in ((0, 1), (1, 0)):
+                self.to_x[first] = [rc(src, dst, (fx, c)) for src, dst in own(first)]
+                self.to_y[second] = [rc(src, dst, (fy, c)) for src, dst in own(second)]
+
+        def relay(self):
+            for copy in self.to_x[0]:
+                copy.wait_recv()
+            self.far_y = rc(self.at(fx, 0), self.at(fx, 0), (fy, c))
+            for copy in self.to_y[1]:
+                copy.wait_recv()
+            self.far_x = rc(self.at(fy, 1), self.at(fy, 1), (fx, c))
+
+        def near(self):
+            for copy in self.to_x[1] + self.to_y[0]:
+                copy.wait_recv()
+
+        def far(self):
+            self.far_y.wait_recv()
+            self.far_x.wait_recv()
+
+    class Scatter:
+        def __init__(self, part, got, last):
+            self.part, self.got, self.last = part, got, last
+
+        def near(self):
+            self.a0 = rc(self.part(fx, 0), self.got(0, 0), (fx, c))
+            self.b0 = rc(self.part(fy, 1), self.got(0, 1), (fy, c))
+
+        def far(self):
+            self.a1 = rc(self.part(fd, 0), self.got(1, 0), (fx, c))
+            self.b1 = rc(self.part(fd, 1), self.got(1, 1), (fy, c))
+
+        def relay(self):
+            self.a1.wait_recv()
+            mine = self.part(fy, 0)
+            mine[...] = (mine[...].astype(F32) + self.got(1, 0)[...].astype(F32)).astype(BF16)
+            self.a2 = rc(mine, self.last(0), (fy, c))
+            self.b1.wait_recv()
+            mine = self.part(fx, 1)
+            mine[...] = (mine[...].astype(F32) + self.got(1, 1)[...].astype(F32)).astype(BF16)
+            self.b2 = rc(mine, self.last(1), (fx, c))
+
+        def wait(self):
+            for copy in (self.a0, self.b0, self.a2, self.b2):
+                copy.wait_recv()
+
+    inner = (z + 1) // 2 == 1
+    outer = jnp.logical_not(inner)
+    toward = (f, 2 * zpeers[0] + h)
+    across = (f, 2 * zpeers[2] + h)
+
+    class Chain:
+        def __init__(self, own, z1, zs, z2, zf):
+            self.own, self.z1, self.zs, self.z2, self.zf = own, z1, zs, z2, zf
+            self.c1 = rc_make(own, z1, toward)
+            self.c2 = rc_make(zs, z2, across)
+            self.c3 = rc_make(zf, zf, toward)
+
+        def first(self):
+            @pl.when(outer)
+            def _():
+                self.c1.start()
+
+        def second(self):
+            @pl.when(inner)
+            def _():
+                self.c1.wait_recv()
+                self.zs[...] = (self.own[...].astype(F32) + self.z1[...].astype(F32)).astype(BF16)
+                self.c2.start()
+
+        def third(self):
+            @pl.when(inner)
+            def _():
+                self.c2.wait_recv()
+                self.zf[...] = (self.zs[...].astype(F32) + self.z2[...].astype(F32)).astype(BF16)
+                self.c3.start()
+
+        def fourth(self):
+            @pl.when(outer)
+            def _():
+                self.c3.wait_recv()
+                self.c1.wait_send()
+
+            @pl.when(inner)
+            def _():
+                self.c2.wait_send()
+                self.c3.wait_send()
+
+            return self.zf
+
+    stacked = jnp.concatenate(
+        [v[...].astype(F32).reshape(1, kr) for v in (v0, v1, v2, v3, v4, v5, v6, v7)], axis=0
+    )
+    PV[f] = stacked
+    for s in range(4):
+        row = seg[s // seq_dev, s % seq_dev : s % seq_dev + 1, :].astype(F32)
+        row = jnp.concatenate([row, jnp.zeros((1, 128 - shard), F32)], axis=1)
+        SEGS[s] = jnp.broadcast_to(row, (8, 128))
+    up_bias = bu[...].astype(F32).reshape(1, wide)
+    bias_up = jnp.where(h == 0, up_bias[:, :hw], up_bias[:, hw:])
+
     barrier = pltpu.get_barrier_semaphore()
     everyone = [(fp, c) for fp in fpeers] + [(f, 2 * zp + h) for zp in zpeers] + [sib]
     for dev in everyone:
         pl.semaphore_signal(barrier, inc=1, device_id=dev, device_id_type=MESH)
     pl.semaphore_wait(barrier, len(everyone))
 
-    def cols(start):
-        return pl.ds(mult(start, 128), hw)
-
-    def krows(j):
-        return pl.ds(mult(j * kr, kr), kr)
-
+    def wq_own_part(i):
+        return [
+            (wq.at[hrows(0, i), cols(b * wide + h * hw)], WQ.at[b, hrows(f, i)]) for b in range(3)
+        ]
+
+    pv_in = [rc(PV.at[f], PV.at[f], (fp, c)) for fp in fpeers]
+    wq_all = Gather(wq_own_part, lambda j, i: WQ.at[:, hrows(j, i), :])
+    my_slot = 4 * h + z
+    s_in = [rc(SEGS.at[zp], SEGR.at[my_slot], (f, 2 * zp + h)) for zp in zpeers]
     x_in = [rc(inp.at[zp], X.at[my_block], (f, 2 * zp + h)) for zp in zpeers]
-    s_in = [rc(seg.at[zp], SEG.at[my_block], (f, 2 * zp + h)) for zp in zpeers]
-    pv_in = [rc(pv, PV.at[f], (fp, c)) for fp in fpeers]
-    wq_in = [
-        rc(wq.at[:, cols(b * wide + h * hw)], WQ.at[b, krows(f)], (fp, c))
-        for b in range(3)
-        for fp in fpeers
-    ]
     cot_block = pl.ds(mult(f * rows_all + h * half + z * shard, shard), shard)
     c_in = [rc(cot.at[zp], COT.at[cot_block], (f, 2 * zp + h)) for zp in zpeers]
     x_own = lc(inp.at[z], X.at[my_block])
-    s_own = lc(seg.at[z], SEG.at[my_block])
-    pv_own = lc(pv, PV.at[f])
     wq_own = [lc(wq.at[:, cols(b * wide + h * hw)], WQ.at[b, krows(f)]) for b in range(3)]
+    wp_own = lc(wp.at[:, cols(h * hw)], WP.at[h, krows(f)])
     c_own = lc(cot.at[z], COT.at[cot_block])
     wd_own = lc(wd.at[pl.ds(mult(h * hw, hw), hw)], WD)
     wu_own = lc(wu.at[:, cols(f * wide + h * hw)], WU.at[krows(f)])
-    wp_own = lc(wp.at[:, cols(h * hw)], WP.at[h, krows(f)])
-
-    x_own.wait()
-    s_own.wait()
-    for copy in x_in + s_in:
-        copy.wait_recv()
-    x_sib = rc(X.at[own_rows], X.at[own_rows], sib)
-    s_sib = rc(SEG.at[own_rows], SEG.at[own_rows], sib)
-    pv_own.wait()
+    SEGR[my_slot] = SEGS[z]
+    SGP[...] = jnp.zeros_like(SGP)
+    GBU[...] = jnp.zeros_like(GBU)
+    wq_all.relay()
+    wp_all = Gather(
+        lambda i: [(wp.at[hrows(0, i), cols(h * hw)], WP.at[h, hrows(f, i)])],
+        lambda j, i: WP.at[h, hrows(j, i)],
+    )
+
     for copy in pv_in:
         copy.wait_recv()
-    vec = PV[0] + PV[1] + PV[2] + PV[3]
-    PV[0] = vec
+    VEC[...] = jnp.concatenate([PV[j] for j in range(4)], axis=1)
 
     def vector(i):
-        return PV[0, i : i + 1, :]
-
-    SGP[...] = jnp.zeros_like(SGP)
-    GBU[...] = jnp.zeros_like(GBU)
-    x_sib.wait_recv()
+        return VEC[i : i + 1, :]
+
+    x_own.wait()
+    for copy in s_in + x_in:
+        copy.wait_recv()
+    my_slots = pl.ds(4 * h, 4)
+    s_sib = rc(SEGR.at[my_slots], SEGR.at[my_slots], sib)
+    x_sib = rc(X.at[own_rows], X.at[own_rows], sib)
+
+    def ln1(start):
+        def block(r):
+            rows = pl.ds(mult(start + r, 64), 64)
+            hat, _ = norm_parts(X[rows, :].astype(F32))
+            H1[rows, :] = (hat * vector(LN1_S) + vector(LN1_B)).astype(BF16)
+
+        loop_rows(half, 64, block)
+
+    ln1(h * half)
     s_sib.wait_recv()
-
-    def ln1(r):
-        hat, _ = norm_parts(X[pl.ds(r, 64), :].astype(F32))
-        H1[pl.ds(r, 64), :] = (hat * vector(LN1_S) + vector(LN1_B)).astype(BF16)
-
-    loop_rows(rows_all, 64, ln1)
+    for b in range(8):
+        turned = jnp.transpose(jnp.broadcast_to(SEGR[b][0:1, :], (128, 128)))
+        SEG[pl.ds(b * shard, shard), :] = turned[:shard, :]
     seg_row = jnp.transpose(SEG[...])[0:1, :]
 
     def mask(r):
-        seg_col = SEG[pl.ds(r, 128), 0:1]
+        rows = pl.ds(r, 128)
+        seg_col = SEG[rows, 0:1]
         place_q = r + lax.broadcasted_iota(jnp.int32, (128, rows_all), 0)
         place_k = lax.broadcasted_iota(jnp.int32, (128, rows_all), 1)
         allowed = (seg_col == seg_row) & ((seg_row >= 0.0) | (place_q == place_k))
-        MB[pl.ds(r, 128), :] = jnp.where(allowed, 0.0, MASKED)
-
+        MB[rows, :] = jnp.where(allowed, 0.0, MASKED)
+
+    x_sib.wait_recv()
+    ln1(o * half)
     loop_rows(rows_all, 128, mask)
-    c_own.wait()
-    for copy in c_in:
-        copy.wait_recv()
-    c_sib = rc(COT.at[chunk_rows(f)], COT.at[chunk_rows(f)], sib)
 
     for copy in wq_own:
         copy.wait()
-    for copy in wq_in:
-        copy.wait_recv()
     wp_own.wait()
-    wp_in = [rc(wp.at[:, cols(h * hw)], WP.at[h, krows(f)], (fp, c)) for fp in fpeers]
+    wq_all.near()
+    wq_all.far()
+    wp_all.relay()
     wu_in = [rc(wu.at[:, cols(fp * wide + h * hw)], WU.at[krows(f)], (fp, c)) for fp in fpeers]
-    cot_in = [rc(COT.at[chunk_rows(f)], COT.at[chunk_rows(f)], (fp, c)) for fp in fpeers]
-    bias_half = [PV[0, i : i + 1, cols(h * hw)] for i in (B_Q, B_V)]
-    pairs = hw // 128
+    bias_half = [
+        jnp.where(h == 0, vector(i)[:, :hw], vector(i)[:, hw:]) for i in (B_Q, B_V)
+    ]
     for b, target in ((0, Q), (1, K), (2, V)):
         prod = dot_nn(H1[...], WQ[b])
         if b == 0:
@@ -658,9 +783,12 @@
         prod = prod.astype(BF16)
         for p in range(pairs):
             target[p] = prod[:, p * 128 : (p + 1) * 128]
-
-    lane = lax.broadcasted_iota(jnp.int32, (1, 128), 1)
-    low_half = lane < 64
+    c_own.wait()
+    for copy in c_in:
+        copy.wait_recv()
+    c_sib = rc(COT.at[chunk_rows(f)], COT.at[chunk_rows(f)], sib)
+
+    low_half = lax.broadcasted_iota(jnp.int32, (1, 128), 1) < 64
 
     def pick(s, values):
         keep = low_half if s == 0 else jnp.logical_not(low_half)
@@ -683,13 +811,18 @@
                 part = dot_nn(low, pick(s, V[p])) * inv
                 total = part if total is None else total + part
             ATT[p, rows, :] = total
-            MIX[3 * h + p, rows, :] = total.astype(BF16)
+            MIX[pairs * h + p, rows, :] = total.astype(BF16)
 
         loop_rows(rows_all, 128, attend)
-        mix_out.append(rc(MIX.at[3 * h + p], MIX.at[3 * h + p], sib))
-
-    for copy in wp_in:
-        copy.wait_recv()
+        mix_out.append(rc(MIX.at[pairs * h + p], MIX.at[pairs * h + p], sib))
+        if p == 0:
+            cot_all = Gather(
+                lambda i: [(COT.at[token_rows(f, i)], COT.at[token_rows(f, i)])],
+                lambda j, i: COT.at[token_rows(j, i)],
+            )
+
+    wp_all.near()
+    wp_all.far()
     wp_sib = rc(WP.at[h], WP.at[h], sib)
     for copy in mix_out:
         copy.wait_recv()
@@ -707,8 +840,12 @@
         ).astype(BF16)
 
     loop_rows(half, 64, project)
-    h2_in = [rc(H2.at[chunk_rows(f)], H2.at[chunk_rows(f)], (fp, c)) for fp in fpeers]
+    h2_all = Gather(
+        lambda i: [(H2.at[token_rows(f, i)], H2.at[token_rows(f, i)])],
+        lambda j, i: H2.at[token_rows(j, i)],
+    )
     h2_sib = rc(H2.at[chunk_rows(f)], H2.at[chunk_rows(f)], sib)
+    cot_all.relay()
 
     for copy in wu_in:
         copy.wait_recv()
@@ -716,7 +853,6 @@
     wd_own.wait()
     c_sib.wait_recv()
     h2_sib.wait_recv()
-    bias_up = bu[h]
 
     def mlp(j):
         def block(r):
@@ -747,100 +883,78 @@
 
         loop_rows(half, 64, block)
 
+    def across_core(buf, j):
+        return rc(buf.at[chunk_rows(j)], buf.at[chunk_rows(j)], sib)
+
     own_pair = mlp(f)
-    fwd = []
-    for i, fp in enumerate(fpeers):
-        cot_in[i].wait_recv()
-        fwd.append(rc(COT.at[chunk_rows(fp)], COT.at[chunk_rows(fp)], sib))
-    h2_fwd = []
+    cot_all.near()
+    cot_fwd = [across_core(COT, fx), across_core(COT, fy)]
+    h2_all.relay()
+    h2_all.near()
+    h2_fwd = [across_core(H2, fx), across_core(H2, fy)]
+    d_plane = Scatter(
+        lambda j, i: PDH.at[token_rows(j, i)],
+        lambda w, i: RDI.at[w, pl.ds(i * (half // 2), half // 2)],
+        lambda i: RDI.at[2, pl.ds(i * (half // 2), half // 2)],
+    )
+    o_plane = Scatter(
+        lambda j, i: PO.at[token_rows(j, i)],
+        lambda w, i: ROI.at[w, pl.ds(i * (half // 2), half // 2)],
+        lambda i: ROI.at[2, pl.ds(i * (half // 2), half // 2)],
+    )
+    cot_fwd[0].wait_recv()
+    h2_fwd[0].wait_recv()
+    x_pair = mlp(fx)
+    cot_all.far()
+    cot_fwd.append(across_core(COT, fd))
+    cot_fwd[1].wait_recv()
+    h2_fwd[1].wait_recv()
+    y_pair = mlp(fy)
+    h2_all.far()
+    h2_fwd.append(across_core(H2, fd))
+    x_pair[0].wait_recv()
+    join(PDH, RDH, fx)
+    y_pair[0].wait_recv()
+    join(PDH, RDH, fy)
+    d_plane.near()
+    cot_fwd[2].wait_recv()
+    h2_fwd[2].wait_recv()
+    d_pair = mlp(fd)
+    own_pair[0].wait_recv()
+    join(PDH, RDH, f)
+    d_pair[0].wait_recv()
+    join(PDH, RDH, fd)
+    d_plane.far()
+    for pair, j in ((own_pair, f), (x_pair, fx), (y_pair, fy), (d_pair, fd)):
+        pair[1].wait_recv()
+        join(PO, RO, j)
+
+    GD[...] = dot_tn(ACT[...], COT[...]).astype(BF16)
+    chain_d, chain_u = [], []
     for i in range(2):
-        h2_in[i].wait_recv()
-        h2_fwd.append(rc(H2.at[chunk_rows(fpeers[i])], H2.at[chunk_rows(fpeers[i])], sib))
-    pairs_out = []
-    dh_in = []
-    for i, fp in enumerate(fpeers):
-        fwd[i].wait_recv()
-        h2_fwd[i].wait_recv()
-        pairs_out.append(mlp(fp))
-        if i == 0:
-            h2_in[2].wait_recv()
-            h2_fwd.append(rc(H2.at[chunk_rows(fpeers[2])], H2.at[chunk_rows(fpeers[2])], sib))
-        pairs_out[i][0].wait_recv()
-        join(PDH, RDH, fp)
-        dh_in.append(rc(PDH.at[chunk_rows(fp)], RDI.at[f], (fp, c)))
-    o_in = []
-    for i, fp in enumerate(fpeers):
-        pairs_out[i][1].wait_recv()
-        join(PO, RO, fp)
-        o_in.append(rc(PO.at[chunk_rows(fp)], ROI.at[f], (fp, c)))
-
-    inner = (z + 1) // 2 == 1
-    outer = jnp.logical_not(inner)
-    toward = (f, 2 * zpeers[0] + h)
-    across = (f, 2 * zpeers[2] + h)
-
-    class Chain:
-        def __init__(self, own, z1, zs, z2, zf):
-            self.own, self.z1, self.zs, self.z2, self.zf = own, z1, zs, z2, zf
-            self.c1 = rc_make(own, z1, toward)
-            self.c2 = rc_make(zs, z2, across)
-            self.c3 = rc_make(zf.at[h], zf.at[h], toward)
-            self.c4 = rc_make(zf.at[h], zf.at[h], sib)
-
-        def first(self):
-            @pl.when(outer)
-            def _():
-                self.c1.start()
-
-        def second(self):
-            @pl.when(inner)
-            def _():
-                self.c1.wait_recv()
-                self.zs[...] = (self.own[...].astype(F32) + self.z1[...].astype(F32)).astype(BF16)
-                self.c2.start()
-
-        def third(self):
-            @pl.when(inner)
-            def _():
-                self.c2.wait_recv()
-                self.zf[h] = (self.zs[...].astype(F32) + self.z2[...].astype(F32)).astype(BF16)
-                self.c3.start()
-
-        def fourth(self):
-            @pl.when(outer)
-            def _():
-                self.c3.wait_recv()
-                self.c1.wait_send()
-
-            @pl.when(inner)
-            def _():
-                self.c2.wait_send()
-                self.c3.wait_send()
-
-            self.c4.start()
-
-        def fifth(self):
-            self.c4.wait_recv()
-            self.c4.wait_send()
-
-    GD[...] = dot_tn(ACT[...], COT[...]).astype(BF16)
-    chain_d = Chain(GD, Z1D, ZSD, Z2D, ZFD)
-    chain_d.first()
+        part = pl.ds(i * (hw // 2), hw // 2)
+        chain_d.append(
+            Chain(GD.at[part], Z1D.at[part], ZSD.at[part], Z2D.at[part], ZFD.at[h, part])
+        )
+        chain_d[i].first()
+    d_plane.relay()
+    o_plane.near()
+    o_plane.far()
     GU[...] = dot_tn(H2[...], DPRE[...]).astype(BF16)
-    gu_in = [rc(GU.at[krows(fp)], RGU.at[f], (fp, c)) for fp in fpeers]
-    RGU[f] = GU[krows(f), :]
+    for i in range(2):
+        part = pl.ds(i * hw, hw)
+        chain_u.append(Chain(GU.at[part], Z1U.at[part], ZSU.at[part], Z2U.at[part], GUZ.at[part]))
+        chain_u[i].first()
     SGP[B_U : B_U + 1, cols(h * hw)] = GBU[...]
 
-    own_pair[0].wait_recv()
-    for copy in dh_in:
-        copy.wait_recv()
+    d_plane.wait()
 
     def ln2_back(r):
         rows = pl.ds(r, 64)
         mine = pl.ds(mult(f * rows_all + h * half + r, 64), 64)
-        d_h2 = PDH[mine, :].astype(F32) + RDH[f, rows, :].astype(F32)
-        for fp in fpeers:
-            d_h2 = d_h2 + RDI[fp, rows, :].astype(F32)
+        d_h2 = PDH[mine, :].astype(F32)
+        for w in (0, 2):
+            d_h2 = d_h2 + RDI[w, rows, :].astype(F32)
         hat, inv = norm_parts(RES[rows, :])
         SGP[LN2_S : LN2_S + 1, :] += jnp.sum(d_h2 * hat, 0, keepdims=True)
         SGP[LN2_B : LN2_B + 1, :] += jnp.sum(d_h2, 0, keepdims=True)
@@ -858,18 +972,24 @@
             DMS[g, rows, :] = d_mixed[:, g * 128 : (g + 1) * 128]
 
     loop_rows(half, 64, ln2_back)
-    dm_sib = rc(DMS.at[pl.ds(3 * o, 3)], DM.at[:, own_rows, :], sib)
+    dm_sib = rc(DMS.at[pl.ds(pairs * o, pairs)], DM.at[:, own_rows, :], sib)
     dbr_sib = rc(DBR.at[o], DBX.at[own_rows], sib)
-    DM[:, own_rows, :] = DMS[pl.ds(3 * h, 3)]
+    DM[:, own_rows, :] = DMS[pl.ds(pairs * h, pairs)]
     DBX[own_rows, :] = DBR[h]
-    chain_d.second()
+    chain_d[0].second()
     dbr_sib.wait_recv()
     mixed_all = jnp.concatenate([MIX[g] for g in range(2 * pairs)], axis=1)
     GPP[...] = dot_tn(mixed_all, DBX[...]).astype(BF16)
-    gp_in = [rc(GPP.at[krows(fp)], RGP.at[f], (fp, c)) for fp in fpeers]
+    p_plane = Scatter(
+        lambda j, i: GPP.at[hrows(j, i)],
+        lambda w, i: RGP.at[w, hrows(0, i)],
+        lambda i: RGP.at[2, hrows(0, i)],
+    )
+    p_plane.far()
+    p_plane.near()
     dm_sib.wait_recv()
 
-    def attention_back(p):
+    def attention_back(p, steps):
         def prepare(r):
             rows = pl.ds(r, 128)
             d_out = DM[p, rows, :].astype(F32)
@@ -879,9 +999,10 @@
                 DLT[s, rows, :] = jnp.sum(scaled.astype(F32) * ATT[p, rows, :], -1, keepdims=True)
 
         loop_rows(rows_all, 128, prepare)
-        here = slice(p * 128, (p + 1) * 128)
         d_value = dot_tn(E[2 * p], DOS[0]) + dot_tn(E[2 * p + 1], DOS[1])
-        DQKV[2, :, here] = d_value.astype(BF16)
+        DQKV[p, :, 256:384] = d_value.astype(BF16)
+        for step in steps[0]:
+            step()
 
         def block(r):
             rows = pl.ds(r, 128)
@@ -894,65 +1015,74 @@
                 E[2 * p + s, rows, :] = d_scores
                 part = dot_nn(d_scores, pick(s, K[p]))
                 d_query = part if d_query is None else d_query + part
-            DQKV[0, rows, here] = (d_query * SCORE_SCALE).astype(BF16)
+            DQKV[p, rows, 0:128] = (d_query * SCORE_SCALE).astype(BF16)
 
         loop_rows(rows_all, 128, block)
+        for step in steps[1]:
+            step()
         d_key = dot_tn(E[2 * p], pick(0, Q[p])) + dot_tn(E[2 * p + 1], pick(1, Q[p]))
-        DQKV[1, :, here] = d_key.astype(BF16)
-
-    attention_back(0)
-    chain_d.third()
-    for copy in gu_in:
-        copy.wait_recv()
-    chain_u = Chain(RGU, Z1U, ZSU, Z2U, ZFU)
-    chain_u.first()
-    attention_back(1)
-    chain_d.fourth()
-    own_pair[1].wait_recv()
-    for copy in o_in:
-        copy.wait_recv()
-
-    def finish(r):
-        rows = pl.ds(r, 64)
-        mine = pl.ds(mult(f * rows_all + h * half + r, 64), 64)
-        total = PO[mine, :].astype(F32) + RO[f, rows, :].astype(F32)
-        for fp in fpeers:
-            total = total + ROI[fp, rows, :].astype(F32)
-        OUTB[rows, :] = (RES[rows, :] + total + vector(B_D)).astype(BF16)
-
-    loop_rows(half, 64, finish)
-
-    def block_of(zp):
-        return pl.ds(mult(zp * shard, shard), shard)
-
-    res_in = [rc(OUTB.at[block_of(zp)], out_ref.at[z], (f, 2 * zp + h)) for zp in zpeers]
-    res_own = lc(OUTB.at[block_of(z)], out_ref.at[z])
-    chain_u.second()
-    for copy in gp_in:
-        copy.wait_recv()
-
-    def owned_sum(own, got):
-        total = own.astype(F32)
-        for fp in fpeers:
-            total = total + got[fp].astype(F32)
-        return total.astype(BF16)
-
-    GP[...] = owned_sum(GPP[krows(f), :], RGP)
-    chain_p = Chain(GP, Z1P, ZSP, Z2P, ZFP)
-    chain_p.first()
-    attention_back(2)
-    chain_u.third()
-    chain_p.second()
-
-    for b in range(3):
-        GQ[b] = dot_tn(H1[...], DQKV[b]).astype(BF16)
-    gq_in = [rc(GQ.at[:, krows(fp), :], RGQ.at[f], (fp, c)) for fp in fpeers]
+        DQKV[p, :, 128:256] = d_key.astype(BF16)
+        GQ[p] = dot_tn(H1[...], DQKV[p]).astype(BF16)
+        plane = Scatter(
+            lambda j, i: GQ.at[p, hrows(j, i)],
+            lambda w, i: RGQ.at[p, w, hrows(0, i)],
+            lambda i: RGQ.at[p, 2, hrows(0, i)],
+        )
+        for step in steps[2]:
+            step()
+        plane.far()
+        plane.near()
+        here = pl.ds(mult(h * hw + p * 128, 128), 128)
+        for b, i in ((0, B_Q), (2, B_V)):
+            SGP[i : i + 1, here] = jnp.sum(
+                DQKV[p, :, b * 128 : (b + 1) * 128].astype(F32), 0, keepdims=True
+            )
+        return plane
+
+    kept = {}
+
+    def finish_out():
+        o_plane.wait()
+
+        def finish(r):
+            rows = pl.ds(r, 64)
+            mine = pl.ds(mult(f * rows_all + h * half + r, 64), 64)
+            total = PO[mine, :].astype(F32)
+            for w in (0, 2):
+                total = total + ROI[w, rows, :].astype(F32)
+            OUTB[rows, :] = (RES[rows, :] + total + vector(B_D)).astype(BF16)
+
+        loop_rows(half, 64, finish)
+        kept["res"] = [rc(OUTB.at[block_of(zp)], out_ref.at[z], (f, 2 * zp + h)) for zp in zpeers]
+        kept["res_own"] = lc(OUTB.at[block_of(z)], out_ref.at[z])
+
+    q_plane = []
+    q_plane.append(
+        attention_back(0, ([chain_d[0].third], [chain_d[1].second], [o_plane.relay]))
+    )
+    q_plane.append(
+        attention_back(1, ([p_plane.relay], [chain_u[0].second, chain_d[1].third], []))
+    )
+    q_plane.append(
+        attention_back(2, ([q_plane[0].relay], [finish_out, chain_u[1].second], [chain_u[0].third]))
+    )
+
+    def joined(b):
+        return jnp.concatenate([DQKV[p, :, b * 128 : (b + 1) * 128] for p in range(pairs)], axis=1)
+
     PD1[...] = (
-        dot_nt(DQKV[0], WQ[0]) + dot_nt(DQKV[1], WQ[1]) + dot_nt(DQKV[2], WQ[2])
+        dot_nt(joined(0), WQ[0]) + dot_nt(joined(1), WQ[1]) + dot_nt(joined(2), WQ[2])
     ).astype(BF16)
     d1_sib = rc(PD1.at[oth_rows], RD1, sib)
-    for b, i in ((0, B_Q), (2, B_V)):
-        SGP[i : i + 1, cols(h * hw)] = jnp.sum(DQKV[b].astype(F32), 0, keepdims=True)
+    zf_d = [chain.fourth() for chain in chain_d]
+    d_sib = rc(ZFD.at[h], ZFD.at[h], sib)
+    q_plane[1].relay()
+    p_plane.wait()
+    GP[...] = (
+        GPP[krows(f), :].astype(F32) + RGP[0].astype(F32) + RGP[2].astype(F32)
+    ).astype(BF16)
+    chain_p = Chain(GP, Z1P, ZSP, Z2P, ZFP.at[h])
+    chain_p.first()
     d1_sib.wait_recv()
 
     def ln1_back(r):
@@ -965,55 +1095,130 @@
         DIN[rows, :] = (DRES[rows, :] + norm_back(d_h1, hat, inv, vector(LN1_S))).astype(BF16)
 
     loop_rows(half, 64, ln1_back)
+    sg_sib = rc(SGP, SGS, sib)
+
+    chain_q = []
+
+    def q_own(b):
+        q_plane[b].wait()
+        GQF[b] = (
+            GQ[b, krows(f), :].astype(F32) + RGQ[b, 0].astype(F32) + RGQ[b, 2].astype(F32)
+        ).astype(BF16)
+        chain_q.append(Chain(GQF.at[b], Z1Q.at[b], ZSQ.at[b], Z2Q.at[b], ZFQ.at[h, b]))
+        chain_q[b].first()
+
+    q_own(0)
     din_in = [rc(DIN.at[block_of(zp)], din_ref.at[z], (f, 2 * zp + h)) for zp in zpeers]
     din_own = lc(DIN.at[block_of(z)], din_ref.at[z])
-    sg_sib = rc(SGP, SGS, sib)
-    chain_u.fourth()
-    chain_p.third()
-    chain_p.fourth()
+    chain_u[1].third()
+    chain_p.second()
     sg_sib.wait_recv()
     SGB[f] = SGP[...] + SGS[...]
     sgf_in = [rc(SGB.at[f], SGB.at[f], (fp, c)) for fp in fpeers]
-
-    for copy in gq_in:
-        copy.wait_recv()
-    for b in range(3):
-        total = GQ[b, krows(f), :].astype(F32)
-        for fp in fpeers:
-            total = total + RGQ[fp, b].astype(F32)
-        GQF[b] = total.astype(BF16)
-    chain_q = Chain(GQF, Z1Q, ZSQ, Z2Q, ZFQ)
-    chain_q.first()
+    q_plane[2].relay()
+    chain_u[0].fourth()
+    chain_p.third()
+    chain_q[0].second()
+    q_own(1)
+    chain_u[1].fourth()
+    gu_out = [rc(GUZ.at[krows(fp)], ZFU.at[h, f], (fp, c)) for fp in fpeers]
+    ZFU[h, f] = GUZ[krows(f), :]
+    chain_q[0].third()
+    chain_q[1].second()
     for copy in sgf_in:
         copy.wait_recv()
     plane = SGB[0] + SGB[1] + SGB[2] + SGB[3]
     row_id = lax.broadcasted_iota(jnp.int32, plane.shape, 0)
     SGZ[z] = jnp.where(row_id == B_U, SGB[f], plane)
     sgz_in = [rc(SGZ.at[z], SGZ.at[z], (f, 2 * zp + h)) for zp in zpeers]
-    chain_q.second()
-    chain_d.fifth()
+    zf_p = chain_p.fourth()
+    p_sib = rc(zf_p, zf_p, sib)
+    q_own(2)
+    chain_q[1].third()
+    chain_q[2].second()
+    d_sib.wait_recv()
     outs = [lc(ZFD.at[k], gd_ref.at[pl.ds(k * hw, hw)]) for k in range(2)]
-    chain_u.fifth()
+    p_sib.wait_recv()
+    outs += [lc(ZFP.at[k], gp_ref.at[:, pl.ds(k * hw, hw)]) for k in range(2)]
+    for copy in gu_out:
+        copy.wait_recv()
+    u_sib = rc(ZFU.at[h], ZFU.at[h], sib)
+    q_sib = []
+    for b in range(2):
+        zf_q = chain_q[b].fourth()
+        q_sib.append(rc(zf_q, zf_q, sib))
+    u_sib.wait_recv()
     outs += [
         lc(ZFU.at[k, s], gu_ref.at[:, pl.ds(s * wide + k * hw, hw)]) for k in range(2) for s in range(4)
     ]
-    chain_p.fifth()
-    outs += [lc(ZFP.at[k], gp_ref.at[:, pl.ds(k * hw, hw)]) for k in range(2)]
-    chain_q.third()
+    chain_q[2].third()
     for copy in sgz_in:
         copy.wait_recv()
     sg_ref[...] = SGZ[0] + SGZ[1] + SGZ[2] + SGZ[3]
-    chain_q.fourth()
-    chain_q.fifth()
-    outs += [
-        lc(ZFQ.at[k, b], gq_ref.at[:, pl.ds(b * wide + k * hw, hw)]) for k in range(2) for b in range(3)
-    ]
-    for copy in res_in + din_in:
+    zf_q = chain_q[2].fourth()
+    q_sib.append(rc(zf_q, zf_q, sib))
+    for p in range(3):
+        q_sib[p].wait_recv()
+        outs += [
+            lc(
+                ZFQ.at[k, p, :, pl.ds(b * 128, 128)],
+                gq_ref.at[:, pl.ds(b * wide + k * hw + p * 128, 128)],
+            )
+            for k in range(2)
+            for b in range(3)
+        ]
+    for copy in kept["res"] + din_in:
         copy.wait_recv()
-    for copy in outs + [res_own, din_own]:
+    for copy in outs + [kept["res_own"], din_own]:
         copy.wait()
     for copy in sent:
         copy.wait_send()
+
+
+def widen_kernel(
+    out_in, din_in, gd_in, gu_in, gp_in, gq_in, sg_hbm,
+    out_ref, din_ref, s0, s1, gq_ref, s2, s3, gp_ref, s4, s5, s6, gu_ref, b_up_ref, gd_ref, s7,
+    sg_in, LT, LD, LU, LP, LQ, FD, FU, FP, FQ, sems,
+):
+    f = lax.axis_index("fsdp")
+    counts = [0]
+
+    def lc(src, dst):
+        copy = pltpu.make_async_copy(src, dst, sems.at[counts[0]])
+        counts[0] += 1
+        copy.start()
+        return copy
+
+    def halves(ref):
+        rows = ref.shape[0] // 2
+        return [pl.ds(i * rows, rows) for i in range(2)]
+
+    small = lc(sg_hbm, sg_in)
+    work = []
+    for src, low, wide, dst in (
+        (gd_in, LD, FD, gd_ref), (gu_in, LU, FU, gu_ref), (gq_in, LQ, FQ, gq_ref), (gp_in, LP, FP, gp_ref)
+    ):
+        for part in halves(src):
+            work.append((lc(src.at[part], low.at[part]), low.at[part], wide.at[part], dst.at[part]))
+    tokens = [lc(out_in, LT.at[0]), lc(din_in, LT.at[1])]
+    passed = []
+    kr = s0.shape[0]
+    small.wait()
+    total = sg_in[0:8, 0:kr]
+    for j in range(1, 4):
+        total = jnp.where(f == j, sg_in[0:8, j * kr : (j + 1) * kr], total)
+    for i, ref in enumerate((s0, s1, s2, s3, s4, s5, s6, s7)):
+        ref[...] = total[i : i + 1, :].reshape(kr)
+    b_up_ref[...] = sg_in[B_U : B_U + 1, :].reshape(sg_in.shape[1])
+    for copy, src, dst in zip(tokens, (LT.at[0], LT.at[1]), (out_ref, din_ref)):
+        copy.wait()
+        passed.append(lc(src, dst))
+    for copy, low, wide, dst in work:
+        copy.wait()
+        wide[...] = low[...].astype(F32)
+        passed.append(lc(wide, dst))
+    for copy in passed:
+        copy.wait()
 
 
 def fast_device(
@@ -1028,71 +1233,74 @@
     kr = wide // 4
     pairs = hw // 128
     heads = 2 * pairs
-    f = lax.axis_index("fsdp")
-    vectors = jnp.stack(
-        (ln1_scale, ln1_bias, b_query, b_value, b_proj, ln2_scale, ln2_bias, b_down)
-    ).astype(F32)
-    spot = lax.broadcasted_iota(jnp.int32, (8, wide), 1) // kr == f
-    packed = jnp.where(spot, jnp.tile(vectors, (1, 4)), 0.0)
-    seg_wide = jnp.broadcast_to(
-        segments.reshape(seqs, shard, 1).astype(F32), (seqs, shard, 128)
-    )
 
     def vm(*shape, dtype=BF16):
         return pltpu.VMEM(shape, dtype)
 
     f32 = functools.partial(vm, dtype=F32)
+    tall = 4 * rows_all
     scratch = [
-        vm(rows_all, wide), f32(rows_all, 128), vm(4 * rows_all, wide), vm(4 * rows_all, wide),
-        f32(4, 8, wide), vm(3, wide, hw), vm(2, wide, hw), vm(wide, hw), vm(hw, wide),
+        vm(rows_all, wide), f32(4, 8, 128), f32(8, 8, 128), f32(rows_all, 128),
+        vm(tall, wide), vm(tall, wide), f32(4, 8, kr), f32(8, wide),
+        vm(3, wide, hw), vm(2, wide, hw), vm(wide, hw), vm(hw, wide),
         vm(rows_all, wide), vm(pairs, rows_all, 128), vm(pairs, rows_all, 128),
         vm(pairs, rows_all, 128), vm(heads, rows_all, rows_all), f32(rows_all, rows_all),
         f32(pairs, rows_all, 128), f32(heads, rows_all, 1), vm(2 * pairs, rows_all, 128),
-        f32(half, wide), vm(4 * rows_all, hw), vm(4 * rows_all, hw),
-        vm(4 * rows_all, wide), vm(4, half, wide), vm(4, half, wide),
-        vm(4 * rows_all, wide), vm(4, half, wide), vm(4, half, wide), vm(half, wide),
+        f32(half, wide),
+        vm(tall, hw), vm(tall, hw),
+        vm(tall, wide), vm(4, half, wide), vm(3, half, wide),
+        vm(tall, wide), vm(4, half, wide), vm(3, half, wide), vm(half, wide),
         f32(half, wide), vm(2, half, hw), vm(rows_all, hw), vm(2 * pairs, half, 128),
         vm(pairs, rows_all, 128), vm(2, rows_all, 128), f32(2, rows_all, 1),
-        vm(3, rows_all, hw),
+        vm(pairs, rows_all, hw),
         vm(hw, wide), vm(hw, wide), vm(hw, wide), vm(hw, wide), vm(2, hw, wide),
-        vm(wide, hw), vm(4, kr, hw), vm(4, kr, hw), vm(4, kr, hw), vm(4, kr, hw), vm(2, 4, kr, hw),
-        vm(wide, hw), vm(4, kr, hw), vm(kr, hw), vm(kr, hw), vm(kr, hw), vm(kr, hw), vm(2, kr, hw),
-        vm(3, wide, hw), vm(4, 3, kr, hw), vm(3, kr, hw), vm(3, kr, hw), vm(3, kr, hw),
-        vm(3, kr, hw), vm(2, 3, kr, hw),
+        vm(wide, hw), vm(wide, hw), vm(wide, hw), vm(wide, hw), vm(wide, hw), vm(2, 4, kr, hw),
+        vm(wide, hw), vm(3, kr, hw), vm(kr, hw), vm(kr, hw), vm(kr, hw), vm(kr, hw), vm(2, kr, hw),
+        vm(pairs, wide, hw), vm(pairs, 3, kr, hw), vm(pairs, kr, hw), vm(pairs, kr, hw),
+        vm(pairs, kr, hw), vm(pairs, kr, hw), vm(2, pairs, kr, hw),
         vm(rows_all, wide), vm(half, wide), vm(half, wide),
-        f32(16, wide), f32(16, wide), f32(4, 16, wide), f32(16, wide), f32(4, 16, wide), f32(1, hw),
-        pltpu.SemaphoreType.DMA((112,)), pltpu.SemaphoreType.DMA((112,)),
-        pltpu.SemaphoreType.DMA((40,)),
+        f32(16, wide), f32(16, wide), f32(4, 16, wide), f32(4, 16, wide), f32(1, hw),
+        pltpu.SemaphoreType.DMA((176,)), pltpu.SemaphoreType.DMA((176,)),
+        pltpu.SemaphoreType.DMA((48,)),
     ]
     hbm = pl.BlockSpec(memory_space=pl.ANY)
     vmem = pl.BlockSpec(memory_space=pltpu.VMEM)
     tokens = jax.ShapeDtypeStruct((seqs, shard, wide), BF16)
+    small = jax.ShapeDtypeStruct((16, wide), F32)
+    grads = (w_down, w_up, w_proj, w_qkv)
     results = pl.pallas_call(
         layer_kernel,
-        out_shape=(
-            tokens, tokens,
-            jax.ShapeDtypeStruct(w_down.shape, BF16), jax.ShapeDtypeStruct(w_up.shape, BF16),
-            jax.ShapeDtypeStruct(w_proj.shape, BF16), jax.ShapeDtypeStruct(w_qkv.shape, BF16),
-            jax.ShapeDtypeStruct((16, wide), F32),
-        ),
-        in_specs=[hbm] * 7 + [vmem, hbm],
+        out_shape=(tokens, tokens) + tuple(jax.ShapeDtypeStruct(w.shape, BF16) for w in grads) + (small,),
+        in_specs=[hbm] + [vmem] * 9 + [hbm] * 4 + [vmem, hbm],
         out_specs=(hbm,) * 6 + (vmem,),
         scratch_shapes=scratch,
         compiler_params=pltpu.CompilerParams(
             collective_id=0, has_side_effects=True, vmem_limit_bytes=62 << 20
         ),
     )(
-        inputs.reshape(tokens.shape), seg_wide, packed, w_qkv, w_proj, w_up, w_down,
-        b_up.astype(F32).reshape(2, 1, hw), cotangent.reshape(tokens.shape),
-    )
-    out, d_input, g_down, g_up, g_proj, g_qkv, small = results
-    mine = lax.dynamic_slice_in_dim(small[:8], f * kr, kr, 1)
-    return (
-        out.reshape(inputs.shape), d_input.reshape(inputs.shape),
-        mine[LN1_S], mine[LN1_B], g_qkv.astype(F32), mine[B_Q], mine[B_V],
-        g_proj.astype(F32), mine[B_P], mine[LN2_S], mine[LN2_B],
-        g_up.astype(F32), small[B_U], g_down.astype(F32), mine[B_D],
-    )
+        inputs.reshape(tokens.shape), segments, ln1_scale, ln1_bias, b_query, b_value, b_proj,
+        ln2_scale, ln2_bias, b_down, w_qkv, w_proj, w_up, w_down, b_up, cotangent.reshape(tokens.shape),
+    )
+    part = jax.ShapeDtypeStruct((kr,), F32)
+
+    def full(w):
+        return jax.ShapeDtypeStruct(w.shape, F32)
+
+    out, d_input, *rest = pl.pallas_call(
+        widen_kernel,
+        out_shape=(
+            tokens, tokens, part, part, full(w_qkv), part, part, full(w_proj), part, part, part,
+            full(w_up), jax.ShapeDtypeStruct((wide,), F32), full(w_down), part,
+        ),
+        in_specs=[pl.BlockSpec(memory_space=pltpu.HBM)] * 7,
+        out_specs=(hbm, hbm, vmem, vmem, hbm, vmem, vmem, hbm, vmem, vmem, vmem, hbm, vmem, hbm, vmem),
+        scratch_shapes=[pltpu.VMEM(small.shape, F32), pltpu.VMEM((2,) + tokens.shape, BF16)]
+        + [pltpu.VMEM(w.shape, BF16) for w in grads]
+        + [pltpu.VMEM(w.shape, F32) for w in grads]
+        + [pltpu.SemaphoreType.DMA((32,))],
+        compiler_params=pltpu.CompilerParams(vmem_limit_bytes=62 << 20),
+    )(*results)
+    return (out.reshape(inputs.shape), d_input.reshape(inputs.shape), *rest)
 
 
 def fits_fast(mesh, inputs, w_up):
@@ -1127,10 +1335,6 @@
         P("fsdp"),
         P(None, "fsdp", "ctx", None),
     )
-    def layer(*args):
-        chosen = fast_device if fits_fast(mesh, args[0], args[11]) else per_device
-        return spread(chosen)(*args)
-
     spread = functools.partial(
         jax.shard_map,
         mesh=mesh,
@@ -1154,4 +1358,9 @@
         ),
         check_vma=False,
     )
+
+    def layer(*args):
+        chosen = fast_device if fits_fast(mesh, args[0], args[11]) else per_device
+        return spread(chosen)(*args)
+
     return layer

time: 246 us -> 167 us (0.68); the launches traced: 242 us -> 166 us
  Pallas kernels: 221 us -> 166 us
  local copies, waits for them, and re-layouts: 11.7 us -> 0 us
  other arithmetic: 8.1 us -> 0 us
    pallas_call x1 -> x2, Pallas kernels: 221 us -> 166 us  [the longest x1 159 us: fast_device(): pl.pallas_call(layer_kernel, out_shape=(tokens, tokens) + tuple((jax.Shap...]
    convert_element_type x5 -> x0, other arithmetic: 7.47 us -> none  [the longest x1 3.03 us: fast_device(): g_up.astype(F32)]
    another operation x11 -> x0, local copies, waits for them, and re-layouts: 5.39 us -> none  [the longest x9 5.3 us: fast_device(): jnp.stack((ln1_scale, ln1_bias, b_query, b_value, b_proj, ln2_scale, ln2_...]
    slice x3 -> x0, local copies, waits for them, and re-layouts: 2.75 us -> none  [the longest x1 1.34 us: fast_device(): small[B_U]]
where the time goes in v2:
time: 167 us; the launch traced here: 166 us
  Pallas kernels  166 us (99%)
    pallas_call x1, Pallas kernels, fast_device(): pl.pallas_call(layer_kernel, out_shape=(tokens, tokens) + tuple((jax.Shap...  159 us
    pallas_call x1, Pallas kernels, fast_device(): pl.pallas_call(widen_kernel, out_shape=(tokens, tokens, part, part, full(...  6.09 us

profile of v2, /device:TPU:1, one launch (start us, length us, event | category | flops | bytes accessed | tf_op | source)
XLA Modules:
  0.0 166.3 jit_solution(5235226521030457895)
XLA Ops:
  0.7 159.4 %shard_map.271 = (bf16[4,64,768]{2,1,0:T(8,128)(2,1)}, bf16[4,64,768]{2,1,0:T(8,128)(2,1)}, bf16[768,768]{1,0:T(8,128)(2,1)}, bf16[192,3072]{1,0:T(8,128)(2,1)},...) custom-call(bf16[4,64,768]{2,1,0:T(8,128)(2,1)} %bitcast.4, s32[2,2,64]{2,1,0:T(2,128)} %seg.1, ...), custom_call_target="tpu_custom_call" | custom-call | tf_op jit(solution)/shard_map/pallas_call | solution.py:1271
  160.1 6.1 %shard_map.272 = (bf16[4,64,768]{2,1,0:T(8,128)(2,1)}, bf16[4,64,768]{2,1,0:T(8,128)(2,1)}, f32[192]{0:T(256)}, f32[192]{0:T(256)}, f32[192,2304]{1,0:T(8,128)},...) custom-call(bf16[4,64,768]{2,1,0:T(8,128)(2,1)} %get-tuple-element.3, ...), custom_call_target="tpu_custom_call" | custom-call | tf_op jit(solution)/shard_map/pallas_call | solution.py:1289

commit v3 on v2

--- a/solution.py
+++ b/solution.py
@@ -470,7 +470,7 @@
 BF16 = jnp.bfloat16
 GELU_A = math.sqrt(2.0 / math.pi)
 GELU_B = 0.044715
-LN1_S, LN1_B, B_Q, B_V, B_P, LN2_S, LN2_B, B_D, B_U = range(9)
+LN1_S, LN1_B, B_Q, B_V, B_P, LN2_S, LN2_B, B_D, B_U, B_U1 = range(10)
 
 
 def dot_nn(left, right):
@@ -515,9 +515,10 @@
     inp, seg, v0, v1, v2, v3, v4, v5, v6, v7, wq, wp, wu, wd, bu, cot,
     out_ref, din_ref, gd_ref, gu_ref, gp_ref, gq_ref, sg_ref,
     X, SEGS, SEGR, SEG, COT, H2, PV, VEC, WQ, WP, WU, WD, H1, Q, K, V, E, MB, ATT, LI, MIX, RES,
-    ACT, DPRE, PDH, RDH, RDI, PO, RO, ROI, OUTB, DRES, DBR, DBX, DMS, DM, DOS, DLT, DQKV,
-    GD, Z1D, ZSD, Z2D, ZFD, GU, Z1U, ZSU, Z2U, GUZ, ZFU, GPP, RGP, GP, Z1P, ZSP, Z2P, ZFP,
-    GQ, RGQ, GQF, Z1Q, ZSQ, Z2Q, ZFQ, PD1, RD1, DIN, SGP, SGS, SGB, SGZ, GBU,
+    ACT, SLOPE, DPRE, PDH, RDH, RDI, PO, RO, ROI, OUTB, DRES, DBR, DBX, DMS, DM, DOS, DLT, DQKV,
+    GD, RGD, GDS, Z1D, ZSD, Z2D, ZFD, GU, RGU, GUS, Z1U, ZSU, Z2U, GUZ, ZFU,
+    GPP, RGP, GP, Z1P, ZSP, Z2P, ZFP,
+    GQ, RGQ, GQF, Z1Q, ZSQ, Z2Q, ZFQ, PD1, RD1, DIN, SGP, SGS, SGT, SGB, SGZ, GBU,
     send_sem, recv_sem, local_sem,
 ):
     f = lax.axis_index("fsdp")
@@ -526,6 +527,10 @@
     h = c % 2
     o = 1 - h
     fx, fy, fd = fpeers = (f + 1 - 2 * (f % 2), (f + 2) % 4, 3 - f)
+    px = f % 2
+    py = f // 2
+    qx = 1 - px
+    qy = 1 - py
     zpeers = (z + 1 - 2 * (z % 2), (z + 2) % 4, 3 - z)
     sib = (f, 2 * z + o)
     seq_dev = seg.shape[1]
@@ -570,6 +575,12 @@
     def chunk_other(j):
         return pl.ds(mult(j * rows_all + o * half, half), half)
 
+    def half_rows(j, core, i):
+        return pl.ds(mult(j * rows_all + core * half + i * (half // 2), half // 2), half // 2)
+
+    def slot(s):
+        return pl.ds(mult(s * hw, hw), hw)
+
     def cols(start):
         return pl.ds(mult(start, 128), hw)
 
@@ -578,9 +589,6 @@
 
     def hrows(j, i):
         return pl.ds(mult(j * kr + i * (kr // 2), kr // 2), kr // 2)
-
-    def token_rows(j, i):
-        return pl.ds(mult(j * rows_all + h * half + i * (half // 2), half // 2), half // 2)
 
     def block_of(zp):
         return pl.ds(mult(zp * shard, shard), shard)
@@ -635,6 +643,26 @@
             for copy in (self.a0, self.b0, self.a2, self.b2):
                 copy.wait_recv()
 
+    class ScatterX:
+        def __init__(self, part, got, last):
+            self.part, self.got, self.last = part, got, last
+
+        def near(self):
+            self.a0 = rc(self.part(fx), self.got(0), (fx, c))
+
+        def far(self):
+            self.a1 = rc(self.part(fd), self.got(1), (fx, c))
+
+        def relay(self):
+            self.a1.wait_recv()
+            mine = self.part(fy)
+            mine[...] = (mine[...].astype(F32) + self.got(1)[...].astype(F32)).astype(BF16)
+            self.a2 = rc(mine, self.last, (fy, c))
+
+        def wait(self):
+            self.a0.wait_recv()
+            self.a2.wait_recv()
+
     inner = (z + 1) // 2 == 1
     outer = jnp.logical_not(inner)
     toward = (f, 2 * zpeers[0] + h)
@@ -682,13 +710,13 @@
     stacked = jnp.concatenate(
         [v[...].astype(F32).reshape(1, kr) for v in (v0, v1, v2, v3, v4, v5, v6, v7)], axis=0
     )
-    PV[f] = stacked
+    up_own = bu[...].astype(F32).reshape(1, wide)
+    up_rows = [up_own[:, i * kr : (i + 1) * kr] for i in range(4)]
+    PV[f] = jnp.concatenate([stacked] + up_rows + [jnp.zeros((4, kr), F32)], axis=0)
     for s in range(4):
         row = seg[s // seq_dev, s % seq_dev : s % seq_dev + 1, :].astype(F32)
         row = jnp.concatenate([row, jnp.zeros((1, 128 - shard), F32)], axis=1)
         SEGS[s] = jnp.broadcast_to(row, (8, 128))
-    up_bias = bu[...].astype(F32).reshape(1, wide)
-    bias_up = jnp.where(h == 0, up_bias[:, :hw], up_bias[:, hw:])
 
     barrier = pltpu.get_barrier_semaphore()
     everyone = [(fp, c) for fp in fpeers] + [(f, 2 * zp + h) for zp in zpeers] + [sib]
@@ -706,14 +734,20 @@
     my_slot = 4 * h + z
     s_in = [rc(SEGS.at[zp], SEGR.at[my_slot], (f, 2 * zp + h)) for zp in zpeers]
     x_in = [rc(inp.at[zp], X.at[my_block], (f, 2 * zp + h)) for zp in zpeers]
-    cot_block = pl.ds(mult(f * rows_all + h * half + z * shard, shard), shard)
-    c_in = [rc(cot.at[zp], COT.at[cot_block], (f, 2 * zp + h)) for zp in zpeers]
+    c_in = [rc(cot.at[zp], COT.at[my_block], (f, 2 * zp + h)) for zp in zpeers]
     x_own = lc(inp.at[z], X.at[my_block])
     wq_own = [lc(wq.at[:, cols(b * wide + h * hw)], WQ.at[b, krows(f)]) for b in range(3)]
     wp_own = lc(wp.at[:, cols(h * hw)], WP.at[h, krows(f)])
-    c_own = lc(cot.at[z], COT.at[cot_block])
-    wd_own = lc(wd.at[pl.ds(mult(h * hw, hw), hw)], WD)
-    wu_own = lc(wu.at[:, cols(f * wide + h * hw)], WU.at[krows(f)])
+    c_own = lc(cot.at[z], COT.at[my_block])
+    wd_own = lc(wd.at[slot(h)], WD.at[slot(py)])
+
+    def wu_strips(x_to):
+        return [
+            (wu.at[:, cols((2 * s + x_to) * wide + h * hw)], WU.at[krows(f), pl.ds(s * hw, hw)])
+            for s in range(2)
+        ]
+
+    wu_own = [lc(src, dst) for src, dst in wu_strips(px)]
     SEGR[my_slot] = SEGS[z]
     SGP[...] = jnp.zeros_like(SGP)
     GBU[...] = jnp.zeros_like(GBU)
@@ -722,10 +756,27 @@
         lambda i: [(wp.at[hrows(0, i), cols(h * hw)], WP.at[h, hrows(f, i)])],
         lambda j, i: WP.at[h, hrows(j, i)],
     )
+    zq = z % 2
+    pair_z = (f, 2 * zpeers[0] + h)
+    wu_x = [
+        rc(
+            wu.at[hrows(0, zq), cols((2 * s + qx) * wide + h * hw)],
+            WU.at[hrows(f, zq), pl.ds(s * hw, hw)],
+            (fx, c),
+        )
+        for s in range(2)
+    ]
+    wu_y = [rc(src, dst, (fy, c)) for src, dst in wu_strips(px)]
 
     for copy in pv_in:
         copy.wait_recv()
     VEC[...] = jnp.concatenate([PV[j] for j in range(4)], axis=1)
+    up_parts = []
+    for s in range(2):
+        shard_vec = PV[2 * s + px]
+        for i in range(2):
+            up_parts.append(jnp.where(h == 0, shard_vec[8 + i : 9 + i], shard_vec[10 + i : 11 + i]))
+    bias_up = jnp.concatenate(up_parts, axis=1)
 
     def vector(i):
         return VEC[i : i + 1, :]
@@ -770,7 +821,6 @@
     wq_all.near()
     wq_all.far()
     wp_all.relay()
-    wu_in = [rc(wu.at[:, cols(fp * wide + h * hw)], WU.at[krows(f)], (fp, c)) for fp in fpeers]
     bias_half = [
         jnp.where(h == 0, vector(i)[:, :hw], vector(i)[:, hw:]) for i in (B_Q, B_V)
     ]
@@ -786,7 +836,8 @@
     c_own.wait()
     for copy in c_in:
         copy.wait_recv()
-    c_sib = rc(COT.at[chunk_rows(f)], COT.at[chunk_rows(f)], sib)
+    c_sib = rc(COT.at[own_rows], COT.at[own_rows], sib)
+    cot_in = rc(COT.at[own_rows], COT.at[chunk_rows(1)], (fx, c))
 
     low_half = lax.broadcasted_iota(jnp.int32, (1, 128), 1) < 64
 
@@ -815,11 +866,12 @@
 
         loop_rows(rows_all, 128, attend)
         mix_out.append(rc(MIX.at[pairs * h + p], MIX.at[pairs * h + p], sib))
-        if p == 0:
-            cot_all = Gather(
-                lambda i: [(COT.at[token_rows(f, i)], COT.at[token_rows(f, i)])],
-                lambda j, i: COT.at[token_rows(j, i)],
-            )
+
+    for copy in wu_x:
+        copy.wait_recv()
+    wu_far = rc(WU.at[hrows(fx, zq)], WU.at[hrows(fx, zq)], (fy, c))
+    wu_pair = [rc(WU.at[hrows(fx, zq)], WU.at[hrows(fx, zq)], pair_z)]
+    wd_in = rc(wd.at[slot(h)], WD.at[slot(py)], (fy, c))
 
     wp_all.near()
     wp_all.far()
@@ -835,46 +887,80 @@
         resid = X[rows, :].astype(F32) + branch + vector(B_P)
         RES[pl.ds(r, 64), :] = resid
         hat, _ = norm_parts(resid)
-        H2[pl.ds(mult(f * rows_all + h * half + r, 64), 64), :] = (
+        H2[rows, :] = (
             hat * vector(LN2_S) + vector(LN2_B)
         ).astype(BF16)
 
     loop_rows(half, 64, project)
-    h2_all = Gather(
-        lambda i: [(H2.at[token_rows(f, i)], H2.at[token_rows(f, i)])],
-        lambda j, i: H2.at[token_rows(j, i)],
-    )
-    h2_sib = rc(H2.at[chunk_rows(f)], H2.at[chunk_rows(f)], sib)
-    cot_all.relay()
-
-    for copy in wu_in:
-        copy.wait_recv()
-    wu_own.wait()
-    wd_own.wait()
-    c_sib.wait_recv()
-    h2_sib.wait_recv()
-
-    def mlp(j):
+    h2_in = [
+        rc(H2.at[half_rows(0, h, i)], H2.at[half_rows(1, h, i)], (fx, c)) for i in range(2)
+    ]
+    h2_sib = rc(H2.at[own_rows], H2.at[own_rows], sib)
+    wu_far.wait_recv()
+    wu_pair.append(rc(WU.at[hrows(fd, zq)], WU.at[hrows(fd, zq)], pair_z))
+
+    def up(start, count):
         def block(r):
-            rows = pl.ds(mult(j * rows_all + r, 128), 128)
+            rows = pl.ds(mult(start + r, 128), 128)
             pre = dot_nn(H2[rows, :], WU[...]) + bias_up
             square = pre * pre
             tan = jnp.tanh(GELU_A * pre * (1.0 + GELU_B * square))
-            low = (0.5 * pre * (1.0 + tan)).astype(BF16)
-            slope = 0.5 * (1.0 + tan) + (0.5 * GELU_A) * pre * (1.0 - tan * tan) * (
+            ACT[rows, :] = (0.5 * pre * (1.0 + tan)).astype(BF16)
+            SLOPE[rows, :] = 0.5 * (1.0 + tan) + (0.5 * GELU_A) * pre * (1.0 - tan * tan) * (
                 1.0 + (3.0 * GELU_B) * square
             )
-            ACT[rows, :] = low
-            d_pre = (dot_nt(COT[rows, :], WD[...]) * slope).astype(BF16)
+
+        loop_rows(count, 128, block)
+
+    def back(start, count):
+        def block(r):
+            rows = pl.ds(mult(start + r, 128), 128)
+            d_pre = (dot_nt(COT[rows, :], WD[...]) * SLOPE[rows, :]).astype(BF16)
             DPRE[rows, :] = d_pre
             GBU[...] += jnp.sum(d_pre.astype(F32), 0, keepdims=True)
             PDH[rows, :] = dot_nt(d_pre, WU[...]).astype(BF16)
-            PO[rows, :] = dot_nn(low, WD[...]).astype(BF16)
-
-        loop_rows(rows_all, 128, block)
-        first = rc(PDH.at[chunk_other(j)], RDH.at[j], sib)
-        second = rc(PO.at[chunk_other(j)], RO.at[j], sib)
-        return first, second
+
+        loop_rows(count, 128, block)
+
+    def start_of(j, core, i):
+        return j * rows_all + core * half + i * (half // 2)
+
+    class Owned:
+        def __init__(self, mine, got, total, copy, z1, zs, z2, zf):
+            self.mine, self.got, self.copy, self.total = mine, got, copy, total
+            self.chain = Chain(total, z1, zs, z2, zf)
+            self.second, self.third, self.fourth = (
+                self.chain.second, self.chain.third, self.chain.fourth
+            )
+
+        def first(self):
+            self.copy.wait_recv()
+            self.total[...] = (self.mine[...].astype(F32) + self.got[...].astype(F32)).astype(BF16)
+            self.chain.first()
+
+    quarter = hw // 4
+
+    def owned(part_of, got, total, z1, zs, z2, zf):
+        made = []
+        for i in range(4):
+            part = pl.ds(i * quarter, quarter)
+
+            def rows(s, i=i):
+                return pl.ds(mult(s * hw + i * quarter, quarter), quarter)
+
+            copy = rc(part_of.at[rows(qy)], got.at[part], (fy, c))
+            made.append(
+                Owned(
+                    part_of.at[rows(py)], got.at[part], total.at[part], copy,
+                    z1.at[part], zs.at[part], z2.at[part], zf.at[part],
+                )
+            )
+        return made
+
+    def down(j):
+        rows = pl.ds(j * rows_all, rows_all)
+        PO[rows, :] = dot_nn(ACT[rows, :], WD[...]).astype(BF16)
+        return rc(PO.at[chunk_other(j)], RO.at[j], sib)
 
     def join(buf, got, j):
         def block(r):
@@ -883,78 +969,72 @@
 
         loop_rows(half, 64, block)
 
-    def across_core(buf, j):
-        return rc(buf.at[chunk_rows(j)], buf.at[chunk_rows(j)], sib)
-
-    own_pair = mlp(f)
-    cot_all.near()
-    cot_fwd = [across_core(COT, fx), across_core(COT, fy)]
-    h2_all.relay()
-    h2_all.near()
-    h2_fwd = [across_core(H2, fx), across_core(H2, fy)]
-    d_plane = Scatter(
-        lambda j, i: PDH.at[token_rows(j, i)],
-        lambda w, i: RDI.at[w, pl.ds(i * (half // 2), half // 2)],
-        lambda i: RDI.at[2, pl.ds(i * (half // 2), half // 2)],
-    )
-    o_plane = Scatter(
-        lambda j, i: PO.at[token_rows(j, i)],
-        lambda w, i: ROI.at[w, pl.ds(i * (half // 2), half // 2)],
-        lambda i: ROI.at[2, pl.ds(i * (half // 2), half // 2)],
-    )
-    cot_fwd[0].wait_recv()
+    for copy in wu_own + [wd_own]:
+        copy.wait()
+    for copy in wu_y + wu_pair + [c_sib, h2_sib]:
+        copy.wait_recv()
+    up(0, rows_all)
+    cot_in.wait_recv()
+    cot_fwd = rc(COT.at[chunk_rows(1)], COT.at[chunk_rows(1)], sib)
+
+    def arrive(i):
+        h2_in[i].wait_recv()
+        return rc(H2.at[half_rows(1, h, i)], H2.at[half_rows(1, h, i)], sib)
+
+    def partial(i):
+        return rc(PDH.at[half_rows(1, o, i)], RDH.at[1, pl.ds(i * (half // 2), half // 2)], sib)
+
+    def pass_on(i, copy):
+        copy.wait_recv()
+        for r in range(0, half // 2, 64):
+            rows = pl.ds(mult(start_of(1, h, i) + r, 64), 64)
+            got = RDH[1, i * (half // 2) + r : i * (half // 2) + r + 64, :]
+            PDH[rows, :] = (PDH[rows, :].astype(F32) + got.astype(F32)).astype(BF16)
+        return rc(PDH.at[half_rows(1, h, i)], RDI.at[pl.ds(i * (half // 2), half // 2)], (fx, c))
+
+    h2_fwd = [arrive(0)]
+    up(start_of(1, h, 0), half // 2)
     h2_fwd[0].wait_recv()
-    x_pair = mlp(fx)
-    cot_all.far()
-    cot_fwd.append(across_core(COT, fd))
-    cot_fwd[1].wait_recv()
+    up(start_of(1, o, 0), half // 2)
+    cot_fwd.wait_recv()
+    wd_in.wait_recv()
+    h2_fwd.append(arrive(1))
+    back(start_of(1, o, 0), half // 2)
+    far_dh = [partial(0)]
+    back(start_of(1, h, 0), half // 2)
     h2_fwd[1].wait_recv()
-    y_pair = mlp(fy)
-    h2_all.far()
-    h2_fwd.append(across_core(H2, fd))
-    x_pair[0].wait_recv()
-    join(PDH, RDH, fx)
-    y_pair[0].wait_recv()
-    join(PDH, RDH, fy)
-    d_plane.near()
-    cot_fwd[2].wait_recv()
-    h2_fwd[2].wait_recv()
-    d_pair = mlp(fd)
-    own_pair[0].wait_recv()
-    join(PDH, RDH, f)
-    d_pair[0].wait_recv()
-    join(PDH, RDH, fd)
-    d_plane.far()
-    for pair, j in ((own_pair, f), (x_pair, fx), (y_pair, fy), (d_pair, fd)):
-        pair[1].wait_recv()
-        join(PO, RO, j)
-
-    GD[...] = dot_tn(ACT[...], COT[...]).astype(BF16)
-    chain_d, chain_u = [], []
-    for i in range(2):
-        part = pl.ds(i * (hw // 2), hw // 2)
-        chain_d.append(
-            Chain(GD.at[part], Z1D.at[part], ZSD.at[part], Z2D.at[part], ZFD.at[h, part])
-        )
-        chain_d[i].first()
-    d_plane.relay()
-    o_plane.near()
-    o_plane.far()
-    GU[...] = dot_tn(H2[...], DPRE[...]).astype(BF16)
-    for i in range(2):
-        part = pl.ds(i * hw, hw)
-        chain_u.append(Chain(GU.at[part], Z1U.at[part], ZSU.at[part], Z2U.at[part], GUZ.at[part]))
-        chain_u[i].first()
-    SGP[B_U : B_U + 1, cols(h * hw)] = GBU[...]
-
-    d_plane.wait()
+    up(start_of(1, o, 1), half // 2)
+    dh_in = [pass_on(0, far_dh[0])]
+    up(start_of(1, h, 1), half // 2)
+    GD[slot(qy), :] = dot_tn(ACT[:, slot(qy)], COT[...]).astype(BF16)
+    chain_d = owned(GD, RGD, GDS, Z1D, ZSD, Z2D, ZFD.at[h])
+    back(start_of(1, o, 1), half // 2)
+    far_dh.append(partial(1))
+    back(start_of(1, h, 1), half // 2)
+    dh_in.append(pass_on(1, far_dh[1]))
+
+    GD[slot(py), :] = dot_tn(ACT[:, slot(py)], COT[...]).astype(BF16)
+    chain_d[0].first()
+    far_o = down(1)
+    back(0, rows_all)
+    own_dh = rc(PDH.at[oth_rows], RDH.at[0], sib)
+    chain_d[1].first()
+    far_o.wait_recv()
+    join(PO, RO, 1)
+    o_in = rc(PO.at[chunk_rows(1)], ROI, (fx, c))
+    GU[slot(qy), :] = dot_tn(H2[:, slot(qy)], DPRE[...]).astype(BF16)
+    chain_u = owned(GU, RGU, GUS, Z1U, ZSU, Z2U, GUZ)
+    chain_z = chain_d + chain_u
+    for s in range(2):
+        SGP[B_U + s : B_U + s + 1, cols(h * hw)] = GBU[:, s * hw : (s + 1) * hw]
+    chain_z[0].second()
+    own_dh.wait_recv()
+
 
     def ln2_back(r):
-        rows = pl.ds(r, 64)
-        mine = pl.ds(mult(f * rows_all + h * half + r, 64), 64)
-        d_h2 = PDH[mine, :].astype(F32)
-        for w in (0, 2):
-            d_h2 = d_h2 + RDI[w, rows, :].astype(F32)
+        rows = pl.ds(mult(r, 64), 64)
+        mine = pl.ds(mult(h * half + r, 64), 64)
+        d_h2 = PDH[mine, :].astype(F32) + RDH[0, rows, :].astype(F32) + RDI[rows, :].astype(F32)
         hat, inv = norm_parts(RES[rows, :])
         SGP[LN2_S : LN2_S + 1, :] += jnp.sum(d_h2 * hat, 0, keepdims=True)
         SGP[LN2_B : LN2_B + 1, :] += jnp.sum(d_h2, 0, keepdims=True)
@@ -971,20 +1051,25 @@
         for g in range(2 * pairs):
             DMS[g, rows, :] = d_mixed[:, g * 128 : (g + 1) * 128]
 
-    loop_rows(half, 64, ln2_back)
+    for i in range(2):
+        dh_in[i].wait_recv()
+        loop_rows(half // 2, 64, lambda r, i=i: ln2_back(i * (half // 2) + r))
     dm_sib = rc(DMS.at[pl.ds(pairs * o, pairs)], DM.at[:, own_rows, :], sib)
     dbr_sib = rc(DBR.at[o], DBX.at[own_rows], sib)
     DM[:, own_rows, :] = DMS[pl.ds(pairs * h, pairs)]
     DBX[own_rows, :] = DBR[h]
-    chain_d[0].second()
+    chain_z[2].first()
+    chain_z[1].second()
+    GU[slot(py), :] = dot_tn(H2[:, slot(py)], DPRE[...]).astype(BF16)
+    own_o = down(0)
+    chain_z[3].first()
+    own_o.wait_recv()
+    join(PO, RO, 0)
+    chain_z[0].third()
     dbr_sib.wait_recv()
     mixed_all = jnp.concatenate([MIX[g] for g in range(2 * pairs)], axis=1)
     GPP[...] = dot_tn(mixed_all, DBX[...]).astype(BF16)
-    p_plane = Scatter(
-        lambda j, i: GPP.at[hrows(j, i)],
-        lambda w, i: RGP.at[w, hrows(0, i)],
-        lambda i: RGP.at[2, hrows(0, i)],
-    )
+    p_plane = ScatterX(lambda j: GPP.at[krows(j)], lambda w: RGP.at[w], RGP.at[2])
     p_plane.far()
     p_plane.near()
     dm_sib.wait_recv()
@@ -1023,11 +1108,16 @@
         d_key = dot_tn(E[2 * p], pick(0, Q[p])) + dot_tn(E[2 * p + 1], pick(1, Q[p]))
         DQKV[p, :, 128:256] = d_key.astype(BF16)
         GQ[p] = dot_tn(H1[...], DQKV[p]).astype(BF16)
-        plane = Scatter(
-            lambda j, i: GQ.at[p, hrows(j, i)],
-            lambda w, i: RGQ.at[p, w, hrows(0, i)],
-            lambda i: RGQ.at[p, 2, hrows(0, i)],
-        )
+        if p < 2:
+            plane = ScatterX(
+                lambda j: GQ.at[p, krows(j)], lambda w: RGQ.at[p, w], RGQ.at[p, 2]
+            )
+        else:
+            plane = Scatter(
+                lambda j, i: GQ.at[p, hrows(j, i)],
+                lambda w, i: RGQ.at[p, w, hrows(0, i)],
+                lambda i: RGQ.at[p, 2, hrows(0, i)],
+            )
         for step in steps[2]:
             step()
         plane.far()
@@ -1042,29 +1132,52 @@
     kept = {}
 
     def finish_out():
-        o_plane.wait()
+        o_in.wait_recv()
 
         def finish(r):
             rows = pl.ds(r, 64)
-            mine = pl.ds(mult(f * rows_all + h * half + r, 64), 64)
-            total = PO[mine, :].astype(F32)
-            for w in (0, 2):
-                total = total + ROI[w, rows, :].astype(F32)
+            mine = pl.ds(mult(h * half + r, 64), 64)
+            total = PO[mine, :].astype(F32) + ROI[rows, :].astype(F32)
             OUTB[rows, :] = (RES[rows, :] + total + vector(B_D)).astype(BF16)
 
         loop_rows(half, 64, finish)
-        kept["res"] = [rc(OUTB.at[block_of(zp)], out_ref.at[z], (f, 2 * zp + h)) for zp in zpeers]
         kept["res_own"] = lc(OUTB.at[block_of(z)], out_ref.at[z])
+
+    def first(i):
+        return chain_z[i].first
+
+    def second(i):
+        return chain_z[i].second
+
+    def third(i):
+        return chain_z[i].third
+
+    kept["res"] = []
+
+    def send_out(i):
+        def send():
+            zp = zpeers[i]
+            kept["res"].append(rc(OUTB.at[block_of(zp)], out_ref.at[z], (f, 2 * zp + h)))
+
+        return send
 
     q_plane = []
     q_plane.append(
-        attention_back(0, ([chain_d[0].third], [chain_d[1].second], [o_plane.relay]))
+        attention_back(
+            0, ([second(2), first(4)], [third(1), second(3)], [first(5), third(2)])
+        )
     )
     q_plane.append(
-        attention_back(1, ([p_plane.relay], [chain_u[0].second, chain_d[1].third], []))
+        attention_back(
+            1,
+            ([second(4), first(6), finish_out, send_out(1)], [third(3), send_out(2)], [second(5), send_out(0)]),
+        )
     )
     q_plane.append(
-        attention_back(2, ([q_plane[0].relay], [finish_out, chain_u[1].second], [chain_u[0].third]))
+        attention_back(
+            2,
+            ([first(7), second(6), p_plane.relay], [third(4)], [third(5), q_plane[0].relay]),
+        )
     )
 
     def joined(b):
@@ -1074,15 +1187,46 @@
         dot_nt(joined(0), WQ[0]) + dot_nt(joined(1), WQ[1]) + dot_nt(joined(2), WQ[2])
     ).astype(BF16)
     d1_sib = rc(PD1.at[oth_rows], RD1, sib)
-    zf_d = [chain.fourth() for chain in chain_d]
-    d_sib = rc(ZFD.at[h], ZFD.at[h], sib)
-    q_plane[1].relay()
-    p_plane.wait()
-    GP[...] = (
-        GPP[krows(f), :].astype(F32) + RGP[0].astype(F32) + RGP[2].astype(F32)
-    ).astype(BF16)
-    chain_p = Chain(GP, Z1P, ZSP, Z2P, ZFP.at[h])
-    chain_p.first()
+    links = []
+
+    def start_chain(mine, z1, zs, z2, zf, pieces):
+        rows = kr // pieces
+        made = []
+        for i in range(pieces):
+            part = pl.ds(i * rows, rows)
+            made.append(Chain(mine.at[part], z1.at[part], zs.at[part], z2.at[part], zf.at[part]))
+            made[i].first()
+        links.append((made, zf))
+
+    def own_p():
+        p_plane.wait()
+        GP[...] = (
+            GPP[krows(f), :].astype(F32) + RGP[0].astype(F32) + RGP[2].astype(F32)
+        ).astype(BF16)
+        start_chain(GP, Z1P, ZSP, Z2P, ZFP.at[h], 1)
+
+    def own_q(b, pieces):
+        q_plane[b].wait()
+        GQF[b] = (
+            GQ[b, krows(f), :].astype(F32) + RGQ[b, 0].astype(F32) + RGQ[b, 2].astype(F32)
+        ).astype(BF16)
+        start_chain(GQF.at[b], Z1Q.at[b], ZSQ.at[b], Z2Q.at[b], ZFQ.at[h, b], pieces)
+
+    def step_two(i):
+        for chain in links[i][0]:
+            chain.second()
+
+    def step_three(i):
+        for chain in links[i][0]:
+            chain.third()
+
+    def step_four(i):
+        for chain in links[i][0]:
+            chain.fourth()
+        return rc(links[i][1], links[i][1], sib)
+
+    second(7)()
+    own_p()
     d1_sib.wait_recv()
 
     def ln1_back(r):
@@ -1096,67 +1240,70 @@
 
     loop_rows(half, 64, ln1_back)
     sg_sib = rc(SGP, SGS, sib)
-
-    chain_q = []
-
-    def q_own(b):
-        q_plane[b].wait()
-        GQF[b] = (
-            GQ[b, krows(f), :].astype(F32) + RGQ[b, 0].astype(F32) + RGQ[b, 2].astype(F32)
-        ).astype(BF16)
-        chain_q.append(Chain(GQF.at[b], Z1Q.at[b], ZSQ.at[b], Z2Q.at[b], ZFQ.at[h, b]))
-        chain_q[b].first()
-
-    q_own(0)
+    third(6)()
+    q_plane[1].relay()
+    own_q(0, 1)
+    step_two(0)
     din_in = [rc(DIN.at[block_of(zp)], din_ref.at[z], (f, 2 * zp + h)) for zp in zpeers]
     din_own = lc(DIN.at[block_of(z)], din_ref.at[z])
-    chain_u[1].third()
-    chain_p.second()
     sg_sib.wait_recv()
-    SGB[f] = SGP[...] + SGS[...]
-    sgf_in = [rc(SGB.at[f], SGB.at[f], (fp, c)) for fp in fpeers]
+    small = SGP[...] + SGS[...]
+    for j in range(4):
+        units = small[B_U + j // 2 : B_U + j // 2 + 1]
+        units = jnp.where(px == j % 2, units, jnp.zeros_like(units))
+        SGT[j] = jnp.concatenate(
+            [small[:8, j * kr : (j + 1) * kr]]
+            + [units[:, i * kr : (i + 1) * kr] for i in range(4)]
+            + [jnp.zeros((4, kr), F32)],
+            axis=0,
+        )
+    SGB[f] = SGT[f]
+    sgf_in = [rc(SGT.at[fp], SGB.at[f], (fp, c)) for fp in fpeers]
     q_plane[2].relay()
-    chain_u[0].fourth()
-    chain_p.third()
-    chain_q[0].second()
-    q_own(1)
-    chain_u[1].fourth()
-    gu_out = [rc(GUZ.at[krows(fp)], ZFU.at[h, f], (fp, c)) for fp in fpeers]
-    ZFU[h, f] = GUZ[krows(f), :]
-    chain_q[0].third()
-    chain_q[1].second()
+    third(7)()
+    own_q(1, 1)
+    step_two(1)
+    step_three(0)
+    for chain in chain_d:
+        chain.fourth()
+    d_sib = rc(ZFD.at[h], ZFD.at[h], sib)
     for copy in sgf_in:
         copy.wait_recv()
-    plane = SGB[0] + SGB[1] + SGB[2] + SGB[3]
-    row_id = lax.broadcasted_iota(jnp.int32, plane.shape, 0)
-    SGZ[z] = jnp.where(row_id == B_U, SGB[f], plane)
+    SGZ[z] = SGB[0] + SGB[1] + SGB[2] + SGB[3]
     sgz_in = [rc(SGZ.at[z], SGZ.at[z], (f, 2 * zp + h)) for zp in zpeers]
-    zf_p = chain_p.fourth()
-    p_sib = rc(zf_p, zf_p, sib)
-    q_own(2)
-    chain_q[1].third()
-    chain_q[2].second()
+    own_q(2, 2)
+    step_two(2)
+    step_three(1)
+    for chain in chain_u:
+        chain.fourth()
+    gu_out = rc(GUZ.at[krows(qx)], ZFU.at[h, px], (fx, c))
+    ZFU[h, px] = GUZ[krows(px), :]
+    p_sib = step_four(0)
     d_sib.wait_recv()
     outs = [lc(ZFD.at[k], gd_ref.at[pl.ds(k * hw, hw)]) for k in range(2)]
-    p_sib.wait_recv()
-    outs += [lc(ZFP.at[k], gp_ref.at[:, pl.ds(k * hw, hw)]) for k in range(2)]
-    for copy in gu_out:
-        copy.wait_recv()
-    u_sib = rc(ZFU.at[h], ZFU.at[h], sib)
-    q_sib = []
-    for b in range(2):
-        zf_q = chain_q[b].fourth()
-        q_sib.append(rc(zf_q, zf_q, sib))
-    u_sib.wait_recv()
-    outs += [
-        lc(ZFU.at[k, s], gu_ref.at[:, pl.ds(s * wide + k * hw, hw)]) for k in range(2) for s in range(4)
-    ]
-    chain_q[2].third()
+    step_two(3)
+    step_three(2)
+    q_sib = [step_four(1)]
     for copy in sgz_in:
         copy.wait_recv()
     sg_ref[...] = SGZ[0] + SGZ[1] + SGZ[2] + SGZ[3]
-    zf_q = chain_q[2].fourth()
-    q_sib.append(rc(zf_q, zf_q, sib))
+    p_sib.wait_recv()
+    outs += [lc(ZFP.at[k], gp_ref.at[:, pl.ds(k * hw, hw)]) for k in range(2)]
+    gu_out.wait_recv()
+    u_sib = rc(ZFU.at[h], ZFU.at[h], sib)
+    step_three(3)
+    q_sib.append(step_four(2))
+    u_sib.wait_recv()
+    outs += [
+        lc(
+            ZFU.at[k, x_of, :, pl.ds(s * hw, hw)],
+            gu_ref.at[:, pl.ds((2 * s + x_of) * wide + k * hw, hw)],
+        )
+        for k in range(2)
+        for s in range(2)
+        for x_of in range(2)
+    ]
+    q_sib.append(step_four(3))
     for p in range(3):
         q_sib[p].wait_recv()
         outs += [
@@ -1180,7 +1327,6 @@
     out_ref, din_ref, s0, s1, gq_ref, s2, s3, gp_ref, s4, s5, s6, gu_ref, b_up_ref, gd_ref, s7,
     sg_in, LT, LD, LU, LP, LQ, FD, FU, FP, FQ, sems,
 ):
-    f = lax.axis_index("fsdp")
     counts = [0]
 
     def lc(src, dst):
@@ -1204,12 +1350,9 @@
     passed = []
     kr = s0.shape[0]
     small.wait()
-    total = sg_in[0:8, 0:kr]
-    for j in range(1, 4):
-        total = jnp.where(f == j, sg_in[0:8, j * kr : (j + 1) * kr], total)
     for i, ref in enumerate((s0, s1, s2, s3, s4, s5, s6, s7)):
-        ref[...] = total[i : i + 1, :].reshape(kr)
-    b_up_ref[...] = sg_in[B_U : B_U + 1, :].reshape(sg_in.shape[1])
+        ref[...] = sg_in[i : i + 1, :].reshape(kr)
+    b_up_ref[...] = jnp.concatenate([sg_in[i : i + 1, :] for i in range(8, 12)], axis=1).reshape(4 * kr)
     for copy, src, dst in zip(tokens, (LT.at[0], LT.at[1]), (out_ref, din_ref)):
         copy.wait()
         passed.append(lc(src, dst))
@@ -1238,35 +1381,37 @@
         return pltpu.VMEM(shape, dtype)
 
     f32 = functools.partial(vm, dtype=F32)
-    tall = 4 * rows_all
+    pair_rows = 2 * rows_all
     scratch = [
         vm(rows_all, wide), f32(4, 8, 128), f32(8, 8, 128), f32(rows_all, 128),
-        vm(tall, wide), vm(tall, wide), f32(4, 8, kr), f32(8, wide),
-        vm(3, wide, hw), vm(2, wide, hw), vm(wide, hw), vm(hw, wide),
+        vm(pair_rows, wide), vm(pair_rows, wide), f32(4, 16, kr), f32(16, wide),
+        vm(3, wide, hw), vm(2, wide, hw), vm(wide, wide), vm(wide, wide),
         vm(rows_all, wide), vm(pairs, rows_all, 128), vm(pairs, rows_all, 128),
         vm(pairs, rows_all, 128), vm(heads, rows_all, rows_all), f32(rows_all, rows_all),
         f32(pairs, rows_all, 128), f32(heads, rows_all, 1), vm(2 * pairs, rows_all, 128),
         f32(half, wide),
-        vm(tall, hw), vm(tall, hw),
-        vm(tall, wide), vm(4, half, wide), vm(3, half, wide),
-        vm(tall, wide), vm(4, half, wide), vm(3, half, wide), vm(half, wide),
+        vm(pair_rows, wide), f32(pair_rows, wide), vm(pair_rows, wide),
+        vm(pair_rows, wide), vm(2, half, wide), vm(half, wide),
+        vm(pair_rows, wide), vm(2, half, wide), vm(half, wide), vm(half, wide),
         f32(half, wide), vm(2, half, hw), vm(rows_all, hw), vm(2 * pairs, half, 128),
         vm(pairs, rows_all, 128), vm(2, rows_all, 128), f32(2, rows_all, 1),
         vm(pairs, rows_all, hw),
-        vm(hw, wide), vm(hw, wide), vm(hw, wide), vm(hw, wide), vm(2, hw, wide),
-        vm(wide, hw), vm(wide, hw), vm(wide, hw), vm(wide, hw), vm(wide, hw), vm(2, 4, kr, hw),
+        vm(wide, wide), vm(hw, wide), vm(hw, wide), vm(hw, wide), vm(hw, wide), vm(hw, wide),
+        vm(2, hw, wide),
+        vm(wide, wide), vm(hw, wide), vm(hw, wide), vm(hw, wide), vm(hw, wide), vm(hw, wide),
+        vm(hw, wide), vm(2, 2, kr, wide),
         vm(wide, hw), vm(3, kr, hw), vm(kr, hw), vm(kr, hw), vm(kr, hw), vm(kr, hw), vm(2, kr, hw),
         vm(pairs, wide, hw), vm(pairs, 3, kr, hw), vm(pairs, kr, hw), vm(pairs, kr, hw),
         vm(pairs, kr, hw), vm(pairs, kr, hw), vm(2, pairs, kr, hw),
         vm(rows_all, wide), vm(half, wide), vm(half, wide),
-        f32(16, wide), f32(16, wide), f32(4, 16, wide), f32(4, 16, wide), f32(1, hw),
-        pltpu.SemaphoreType.DMA((176,)), pltpu.SemaphoreType.DMA((176,)),
-        pltpu.SemaphoreType.DMA((48,)),
+        f32(16, wide), f32(16, wide), f32(4, 16, kr), f32(4, 16, kr), f32(4, 16, kr), f32(1, wide),
+        pltpu.SemaphoreType.DMA((216,)), pltpu.SemaphoreType.DMA((216,)),
+        pltpu.SemaphoreType.DMA((64,)),
     ]
     hbm = pl.BlockSpec(memory_space=pl.ANY)
     vmem = pl.BlockSpec(memory_space=pltpu.VMEM)
     tokens = jax.ShapeDtypeStruct((seqs, shard, wide), BF16)
-    small = jax.ShapeDtypeStruct((16, wide), F32)
+    small = jax.ShapeDtypeStruct((16, kr), F32)
     grads = (w_down, w_up, w_proj, w_qkv)
     results = pl.pallas_call(
         layer_kernel,

time: 167 us -> 148 us (0.89)
  Pallas kernels: 166 us -> 147 us
    pallas_call x1, Pallas kernels: 159 us -> 141 us  [fast_device(): pl.pallas_call(layer_kernel, out_shape=(tokens, tokens) + tuple((jax.Shap...]
where the time goes in v3:
time: 148 us
  Pallas kernels  147 us (99%)
    pallas_call x1, Pallas kernels, fast_device(): pl.pallas_call(layer_kernel, out_shape=(tokens, tokens) + tuple((jax.Shap...  141 us
    pallas_call x1, Pallas kernels, fast_device(): pl.pallas_call(widen_kernel, out_shape=(tokens, tokens, part, part, full(...  6.07 us

profile of v3, /device:TPU:1, one launch (start us, length us, event | category | flops | bytes accessed | tf_op | source)
XLA Modules:
  0.0 147.9 jit_solution(6164916353058163469)
XLA Ops:
  0.7 141.0 %shard_map.271 = (bf16[4,64,768]{2,1,0:T(8,128)(2,1)}, bf16[4,64,768]{2,1,0:T(8,128)(2,1)}, bf16[768,768]{1,0:T(8,128)(2,1)}, bf16[192,3072]{1,0:T(8,128)(2,1)},...) custom-call(bf16[4,64,768]{2,1,0:T(8,128)(2,1)} %bitcast.4, s32[2,2,64]{2,1,0:T(2,128)} %seg.1, ...), custom_call_target="tpu_custom_call" | custom-call | tf_op jit(solution)/shard_map/pallas_call | solution.py:1416
  141.7 6.1 %shard_map.272 = (bf16[4,64,768]{2,1,0:T(8,128)(2,1)}, bf16[4,64,768]{2,1,0:T(8,128)(2,1)}, f32[192]{0:T(256)}, f32[192]{0:T(256)}, f32[192,2304]{1,0:T(8,128)},...) custom-call(bf16[4,64,768]{2,1,0:T(8,128)(2,1)} %get-tuple-element.3, ...), custom_call_target="tpu_custom_call" | custom-call | tf_op jit(solution)/shard_map/pallas_call | solution.py:1434

commit v4 on v3

--- a/solution.py
+++ b/solution.py
@@ -1239,13 +1239,13 @@
         DIN[rows, :] = (DRES[rows, :] + norm_back(d_h1, hat, inv, vector(LN1_S))).astype(BF16)
 
     loop_rows(half, 64, ln1_back)
+    din_in = [rc(DIN.at[block_of(zp)], din_ref.at[z], (f, 2 * zp + h)) for zp in zpeers]
+    din_own = lc(DIN.at[block_of(z)], din_ref.at[z])
     sg_sib = rc(SGP, SGS, sib)
     third(6)()
     q_plane[1].relay()
     own_q(0, 1)
     step_two(0)
-    din_in = [rc(DIN.at[block_of(zp)], din_ref.at[z], (f, 2 * zp + h)) for zp in zpeers]
-    din_own = lc(DIN.at[block_of(z)], din_ref.at[z])
     sg_sib.wait_recv()
     small = SGP[...] + SGS[...]
     for j in range(4):
@@ -1271,13 +1271,13 @@
         copy.wait_recv()
     SGZ[z] = SGB[0] + SGB[1] + SGB[2] + SGB[3]
     sgz_in = [rc(SGZ.at[z], SGZ.at[z], (f, 2 * zp + h)) for zp in zpeers]
-    own_q(2, 2)
-    step_two(2)
-    step_three(1)
     for chain in chain_u:
         chain.fourth()
     gu_out = rc(GUZ.at[krows(qx)], ZFU.at[h, px], (fx, c))
     ZFU[h, px] = GUZ[krows(px), :]
+    own_q(2, 2)
+    step_two(2)
+    step_three(1)
     p_sib = step_four(0)
     d_sib.wait_recv()
     outs = [lc(ZFD.at[k], gd_ref.at[pl.ds(k * hw, hw)]) for k in range(2)]

time: 148 us -> 146 us (0.986)
  Pallas kernels: 147 us -> 145 us
    pallas_call x1, Pallas kernels: 141 us -> 139 us  [fast_device(): pl.pallas_call(layer_kernel, out_shape=(tokens, tokens) + tuple((jax.Shap...]
where the time goes in v4:
time: 146 us
  Pallas kernels  145 us (99%)
    pallas_call x1, Pallas kernels, fast_device(): pl.pallas_call(layer_kernel, out_shape=(tokens, tokens) + tuple((jax.Shap...  139 us
    pallas_call x1, Pallas kernels, fast_device(): pl.pallas_call(widen_kernel, out_shape=(tokens, tokens, part, part, full(...  6.07 us

profile of v4, /device:TPU:1, one launch (start us, length us, event | category | flops | bytes accessed | tf_op | source)
XLA Modules:
  0.0 145.8 jit_solution(2823001789043182847)
XLA Ops:
  0.7 138.9 %shard_map.271 = (bf16[4,64,768]{2,1,0:T(8,128)(2,1)}, bf16[4,64,768]{2,1,0:T(8,128)(2,1)}, bf16[768,768]{1,0:T(8,128)(2,1)}, bf16[192,3072]{1,0:T(8,128)(2,1)},...) custom-call(bf16[4,64,768]{2,1,0:T(8,128)(2,1)} %bitcast.4, s32[2,2,64]{2,1,0:T(2,128)} %seg.1, ...), custom_call_target="tpu_custom_call" | custom-call | tf_op jit(solution)/shard_map/pallas_call | solution.py:1416
  139.5 6.1 %shard_map.272 = (bf16[4,64,768]{2,1,0:T(8,128)(2,1)}, bf16[4,64,768]{2,1,0:T(8,128)(2,1)}, f32[192]{0:T(256)}, f32[192]{0:T(256)}, f32[192,2304]{1,0:T(8,128)},...) custom-call(bf16[4,64,768]{2,1,0:T(8,128)(2,1)} %get-tuple-element.3, ...), custom_call_target="tpu_custom_call" | custom-call | tf_op jit(solution)/shard_map/pallas_call | solution.py:1434

commit v5 on v4

--- a/solution.py
+++ b/solution.py
@@ -707,6 +707,10 @@
 
             return self.zf
 
+    barrier = pltpu.get_barrier_semaphore()
+    everyone = [(fp, c) for fp in fpeers] + [(f, 2 * zp + h) for zp in zpeers] + [sib]
+    for dev in everyone:
+        pl.semaphore_signal(barrier, inc=1, device_id=dev, device_id_type=MESH)
     stacked = jnp.concatenate(
         [v[...].astype(F32).reshape(1, kr) for v in (v0, v1, v2, v3, v4, v5, v6, v7)], axis=0
     )
@@ -718,10 +722,11 @@
         row = jnp.concatenate([row, jnp.zeros((1, 128 - shard), F32)], axis=1)
         SEGS[s] = jnp.broadcast_to(row, (8, 128))
 
-    barrier = pltpu.get_barrier_semaphore()
-    everyone = [(fp, c) for fp in fpeers] + [(f, 2 * zp + h) for zp in zpeers] + [sib]
-    for dev in everyone:
-        pl.semaphore_signal(barrier, inc=1, device_id=dev, device_id_type=MESH)
+    SGP[...] = jnp.zeros_like(SGP)
+    GBU[...] = jnp.zeros_like(GBU)
+    x_own = lc(inp.at[z], X.at[my_block])
+    wq_own = [lc(wq.at[:, cols(b * wide + h * hw)], WQ.at[b, krows(f)]) for b in range(3)]
+    wp_own = lc(wp.at[:, cols(h * hw)], WP.at[h, krows(f)])
     pl.semaphore_wait(barrier, len(everyone))
 
     def wq_own_part(i):
@@ -735,9 +740,6 @@
     s_in = [rc(SEGS.at[zp], SEGR.at[my_slot], (f, 2 * zp + h)) for zp in zpeers]
     x_in = [rc(inp.at[zp], X.at[my_block], (f, 2 * zp + h)) for zp in zpeers]
     c_in = [rc(cot.at[zp], COT.at[my_block], (f, 2 * zp + h)) for zp in zpeers]
-    x_own = lc(inp.at[z], X.at[my_block])
-    wq_own = [lc(wq.at[:, cols(b * wide + h * hw)], WQ.at[b, krows(f)]) for b in range(3)]
-    wp_own = lc(wp.at[:, cols(h * hw)], WP.at[h, krows(f)])
     c_own = lc(cot.at[z], COT.at[my_block])
     wd_own = lc(wd.at[slot(h)], WD.at[slot(py)])
 
@@ -749,8 +751,6 @@
 
     wu_own = [lc(src, dst) for src, dst in wu_strips(px)]
     SEGR[my_slot] = SEGS[z]
-    SGP[...] = jnp.zeros_like(SGP)
-    GBU[...] = jnp.zeros_like(GBU)
     wq_all.relay()
     wp_all = Gather(
         lambda i: [(wp.at[hrows(0, i), cols(h * hw)], WP.at[h, hrows(f, i)])],
@@ -1336,8 +1336,8 @@
         return copy
 
     def halves(ref):
-        rows = ref.shape[0] // 2
-        return [pl.ds(i * rows, rows) for i in range(2)]
+        rows = ref.shape[0] // 4
+        return [pl.ds(i * rows, rows) for i in range(4)]
 
     small = lc(sg_hbm, sg_in)
     work = []
@@ -1442,7 +1442,7 @@
         scratch_shapes=[pltpu.VMEM(small.shape, F32), pltpu.VMEM((2,) + tokens.shape, BF16)]
         + [pltpu.VMEM(w.shape, BF16) for w in grads]
         + [pltpu.VMEM(w.shape, F32) for w in grads]
-        + [pltpu.SemaphoreType.DMA((32,))],
+        + [pltpu.SemaphoreType.DMA((48,))],
         compiler_params=pltpu.CompilerParams(vmem_limit_bytes=62 << 20),
     )(*results)
     return (out.reshape(inputs.shape), d_input.reshape(inputs.shape), *rest)

time: 146 us -> 146 us (level)
  no operation moved by 1% of the time
where the time goes in v5:
time: 146 us
  Pallas kernels  145 us (99%)
    pallas_call x1, Pallas kernels, fast_device(): pl.pallas_call(layer_kernel, out_shape=(tokens, tokens) + tuple((jax.Shap...  139 us
    pallas_call x1, Pallas kernels, fast_device(): pl.pallas_call(widen_kernel, out_shape=(tokens, tokens, part, part, full(...  6.21 us

profile of v5, /device:TPU:1, one launch (start us, length us, event | category | flops | bytes accessed | tf_op | source)
XLA Modules:
  0.0 145.8 jit_solution(9955307411372250094)
XLA Ops:
  0.7 138.8 %shard_map.271 = (bf16[4,64,768]{2,1,0:T(8,128)(2,1)}, bf16[4,64,768]{2,1,0:T(8,128)(2,1)}, bf16[768,768]{1,0:T(8,128)(2,1)}, bf16[192,3072]{1,0:T(8,128)(2,1)},...) custom-call(bf16[4,64,768]{2,1,0:T(8,128)(2,1)} %bitcast.4, s32[2,2,64]{2,1,0:T(2,128)} %seg.1, ...), custom_call_target="tpu_custom_call" | custom-call | tf_op jit(solution)/shard_map/pallas_call | solution.py:1416
  139.5 6.2 %shard_map.272 = (bf16[4,64,768]{2,1,0:T(8,128)(2,1)}, bf16[4,64,768]{2,1,0:T(8,128)(2,1)}, f32[192]{0:T(256)}, f32[192]{0:T(256)}, f32[192,2304]{1,0:T(8,128)},...) custom-call(bf16[4,64,768]{2,1,0:T(8,128)(2,1)} %get-tuple-element.3, ...), custom_call_target="tpu_custom_call" | custom-call | tf_op jit(solution)/shard_map/pallas_call | solution.py:1434
